TPU v7x, 128 devices: a whole 4x4x4 slice. The times are simulated.
128 devices in a mesh: ctx: 8 (over x, y_lo), ffn: 16 (over z, y_hi, core).
Axes of the slice: x: 4, y: 4 (y_hi: 2, y_lo: 2; y = y_hi * 2 + y_lo), z: 4, core: 2. Of those that a mesh axis runs over, the one named last changes fastest.
Arguments:
- resid_in: bfloat16 [1024, 4096], P(('ctx', 'ffn')), may hold values from -6 to 6
- queries: bfloat16 [1024, 4096], P('ctx', 'ffn'), may hold values from -6 to 6
- keys_in: bfloat16 [1024, 1024], P('ctx'), may hold values from -6 to 6
- value_rows_input: bfloat16 [1024, 1024], P('ctx'), may hold values from -6 to 6
- w_out: bfloat16 [4096, 4096], P('ffn'), may hold values from -0.09375 to 0.09375
- norm_gain: float32 [4096], replicated, may hold values from 0.5 to 1.5
- w_gate: bfloat16 [4096, 7168], P(None, 'ffn'), may hold values from -0.09375 to 0.09375
- w_up: bfloat16 [4096, 7168], P(None, 'ffn'), may hold values from -0.09375 to 0.09375
- w_down: bfloat16 [7168, 4096], P('ffn'), may hold values from -0.0625 to 0.0625
- cotangent: bfloat16 [1024, 4096], P(('ctx', 'ffn')), may hold values from -6 to 6
- positions: int32 [1024], P('ctx'), may hold values from 0 to 1023, as said below
- doc_ids: int32 [1024], replicated, may hold values from 0 to 3, never falling along the last dimension, each value on 1 to 512 neighbouring positions
Outputs:
- mixed: bfloat16 [1024, 4096], P(('ctx', 'ffn'))
- grad_resid: bfloat16 [1024, 4096], P(('ctx', 'ffn'))
- grad_queries: bfloat16 [1024, 4096], P('ctx', 'ffn')
- key_gradient_rows: float32 [1024, 1024], P(('ctx', 'ffn'))
- value_gradient_rows: float32 [1024, 1024], P(('ctx', 'ffn'))
- grad_gain: float32 [4096], replicated
- grad_w_out: float32 [4096, 4096], P('ffn', 'ctx')
- grad_w_gate: float32 [4096, 7168], P('ctx', 'ffn')
- grad_w_up: float32 [4096, 7168], P('ctx', 'ffn')
- grad_w_down: float32 [7168, 4096], P('ffn', 'ctx')
Inputs may be any that keep to these rules, and one draw needn't show every extreme that they name: Each aligned block of 64 rows holds 64 consecutive positions in rising order, and every position occurs once.
All inputs are finite; a program needn't handle non-finite values.
Results may differ from a plain program's by a relative error of at most 0.033.
Values may be sent and summed in bfloat16 or wider, within the bound.
A program may use at most 128 MiB of HBM per device.

v0:
```python
import math

import jax
import jax.numpy as jnp
from jax import lax
from jax.sharding import PartitionSpec as P

QUERY_HEADS = 32
KEY_VALUE_HEADS = 8
HEAD_WIDTH = 128


masked_fill = -1e30
norm_eps = 1e-05


def passed_along(value, axis, by):
    count = lax.axis_size(axis)
    return lax.ppermute(value, axis, [(i, (i + by) % count) for i in range(count)])


def tile_visible(query_pos, query_seg, key_pos, key_seg):
    return (key_pos[None, :] <= query_pos[:, None]) & (key_seg[None, :] == query_seg[:, None])


def forward_tile(folded, q_heads, key_piece, value_piece, visible, score_scale):
    row_max, row_total, accumulated = folded
    scores = (
        jnp.einsum("rhd,kd->hrk", q_heads, key_piece, preferred_element_type=jnp.float32)
        * score_scale
    )
    scores = jnp.where(visible[None], scores, masked_fill)
    new_max = jnp.maximum(row_max, jnp.max(scores, axis=2))
    weights = jnp.where(visible[None], jnp.exp(scores - new_max[:, :, None]), 0.0)
    shrink = jnp.exp(row_max - new_max)
    new_total = row_total * shrink + jnp.sum(weights, axis=2)
    product = jnp.einsum(
        "hrk,kd->hrd", weights.astype(jnp.bfloat16), value_piece, preferred_element_type=jnp.float32
    )
    return (new_max, new_total, accumulated * shrink[:, :, None] + product)


def row_contract(left_rows, right_rows):
    return jnp.einsum("rd,rf->df", left_rows, right_rows, preferred_element_type=jnp.float32)


def body(
    resid_in,
    queries,
    keys_in,
    value_rows_input,
    w_out,
    norm_gain,
    w_gate,
    w_up,
    w_down,
    cotangent,
    positions,
    doc_ids,
):
    row_count = queries.shape[0]
    resident_heads = queries.shape[1] // HEAD_WIDTH
    ctx_size = lax.axis_size("ctx")
    ctx_index = lax.axis_index("ctx")
    key_value_group = lax.axis_index("ffn") * resident_heads // (QUERY_HEADS // KEY_VALUE_HEADS)
    score_scale = 1.0 / math.sqrt(HEAD_WIDTH)
    all_pos = lax.all_gather(positions, "ctx", axis=0, tiled=True)
    all_seg = doc_ids[all_pos]
    own_seg = doc_ids[positions]
    key_own = lax.dynamic_slice_in_dim(keys_in, key_value_group * HEAD_WIDTH, HEAD_WIDTH, 1)
    value_own = lax.dynamic_slice_in_dim(
        value_rows_input, key_value_group * HEAD_WIDTH, HEAD_WIDTH, 1
    )
    kv_pair = jnp.stack((key_own, value_own), axis=1)
    q_heads = queries.reshape(row_count, resident_heads, HEAD_WIDTH)

    def key_visible(row_start, row_num):
        return tile_visible(
            positions,
            own_seg,
            lax.dynamic_slice_in_dim(all_pos, row_start, row_num, 0),
            lax.dynamic_slice_in_dim(all_seg, row_start, row_num, 0),
        )

    def fold_keys(folded, shard_rows, row_start):
        visible = key_visible(row_start, shard_rows.shape[0])
        return forward_tile(
            folded, q_heads, shard_rows[:, 0], shard_rows[:, 1], visible, score_scale
        )

    start_state = (
        jnp.full((resident_heads, row_count), masked_fill, jnp.float32),
        jnp.zeros((resident_heads, row_count), jnp.float32),
        jnp.zeros((resident_heads, row_count, HEAD_WIDTH), jnp.float32),
    )

    def pass_step(turn_index, running):
        folded, travel = running
        travel = passed_along(travel, "ctx", 1)
        source = (ctx_index - turn_index - 1) % ctx_size
        return (fold_keys(folded, travel, source * row_count), travel)

    first_state = fold_keys(start_state, kv_pair, ctx_index * row_count)
    (row_max, row_total, accumulated), unused = lax.fori_loop(
        0, ctx_size - 1, pass_step, (first_state, kv_pair)
    )
    attended = (accumulated / row_total[:, :, None]).astype(jnp.bfloat16)
    log_totals = row_max + jnp.log(row_total)
    attended_rows = jnp.transpose(attended, (1, 0, 2)).reshape(
        row_count, resident_heads * HEAD_WIDTH
    )
    projected = lax.psum_scatter(
        jnp.dot(attended_rows, w_out, preferred_element_type=jnp.float32).astype(jnp.bfloat16),
        "ffn",
        scatter_dimension=0,
        tiled=True,
    ).astype(jnp.float32)
    hidden_bf = (resid_in.astype(jnp.float32) + projected).astype(jnp.bfloat16)
    hidden_f = lax.optimization_barrier(hidden_bf).astype(jnp.float32)
    inv_rms = lax.rsqrt(jnp.mean(hidden_f * hidden_f, axis=1, keepdims=True) + norm_eps)
    normed = (hidden_f * inv_rms * norm_gain).astype(jnp.bfloat16)
    normed_rows = lax.all_gather(normed, "ffn", axis=0, tiled=True)
    gate_pre = jnp.dot(normed_rows, w_gate, preferred_element_type=jnp.float32)
    up_proj = jnp.dot(normed_rows, w_up, preferred_element_type=jnp.float32)
    gate_sig = jax.nn.sigmoid(gate_pre)
    activated = (gate_pre * gate_sig * up_proj).astype(jnp.bfloat16)
    mixed = (
        hidden_f
        + lax.psum_scatter(
            jnp.dot(activated, w_down, preferred_element_type=jnp.float32).astype(jnp.bfloat16),
            "ffn",
            scatter_dimension=0,
            tiled=True,
        ).astype(jnp.float32)
    ).astype(jnp.bfloat16)
    cot_rows = lax.all_gather(cotangent, "ffn", axis=0, tiled=True)
    grad_act = jnp.dot(cot_rows, w_down.T, preferred_element_type=jnp.float32)
    grad_up = (grad_act * gate_pre * gate_sig).astype(jnp.bfloat16)
    grad_gate = (grad_act * up_proj * gate_sig * (1.0 + gate_pre * (1.0 - gate_sig))).astype(
        jnp.bfloat16
    )
    grad_normed = lax.psum_scatter(
        (
            jnp.dot(grad_gate, w_gate.T, preferred_element_type=jnp.float32)
            + jnp.dot(grad_up, w_up.T, preferred_element_type=jnp.float32)
        ).astype(jnp.bfloat16),
        "ffn",
        scatter_dimension=0,
        tiled=True,
    ).astype(jnp.float32)
    gained = grad_normed * norm_gain
    inv_cube = inv_rms * inv_rms * inv_rms
    grad_resid = (
        cotangent.astype(jnp.float32)
        + inv_rms * gained
        - hidden_f * inv_cube * jnp.mean(gained * hidden_f, axis=1, keepdims=True)
    ).astype(jnp.bfloat16)
    grad_gain = lax.psum(jnp.sum(grad_normed * hidden_f * inv_rms, axis=0), ("ctx", "ffn"))
    grad_rows = lax.all_gather(grad_resid, "ffn", axis=0, tiled=True)
    grad_attended = jnp.dot(grad_rows, w_out.T, preferred_element_type=jnp.float32).astype(
        jnp.bfloat16
    )
    grad_heads = grad_attended.reshape(row_count, resident_heads, HEAD_WIDTH)
    deltas = jnp.sum(
        grad_heads.astype(jnp.float32)
        * attended_rows.reshape(row_count, resident_heads, HEAD_WIDTH).astype(jnp.float32),
        axis=2,
    )
    delta_heads = deltas.T
    stats_all, deltas_all = (
        lax.all_gather(log_totals.T, "ctx", axis=0, tiled=True),
        lax.all_gather(deltas, "ctx", axis=0, tiled=True),
    )
    shard_rows = lax.all_gather(kv_pair, "ctx", axis=0, tiled=True)
    key_piece = shard_rows[:, 0]
    value_piece = shard_rows[:, 1]
    visible = key_visible(jnp.int32(0), shard_rows.shape[0])

    def update(running):
        scores = (
            jnp.einsum("rhd,kd->hrk", q_heads, key_piece, preferred_element_type=jnp.float32)
            * score_scale
        )
        scores = jnp.where(visible[None], scores, masked_fill)
        prob_weights = jnp.where(visible[None], jnp.exp(scores - log_totals[:, :, None]), 0.0)
        grad_probs = jnp.einsum(
            "rhd,kd->hrk", grad_heads, value_piece, preferred_element_type=jnp.float32
        )
        grad_scores = (prob_weights * (grad_probs - delta_heads[:, :, None])).astype(jnp.bfloat16)
        return (
            jnp.einsum("hrk,kd->rhd", grad_scores, key_piece, preferred_element_type=jnp.float32)
            * score_scale
        )

    grad_query = update(jnp.zeros((row_count, resident_heads, HEAD_WIDTH), jnp.float32))
    zero_block = jnp.zeros((row_count, HEAD_WIDTH), jnp.float32)
    shard_rows = (
        lax.all_gather(queries, "ctx", axis=0, tiled=True),
        lax.all_gather(grad_attended, "ctx", axis=0, tiled=True),
    )
    row_num = shard_rows[0].shape[0]
    q_piece = shard_rows[0].reshape(row_num, resident_heads, HEAD_WIDTH)
    g_piece = shard_rows[1].reshape(row_num, resident_heads, HEAD_WIDTH)
    fold_visible = tile_visible(all_pos, all_seg, positions, own_seg)
    stat_piece = stats_all.T
    delta_piece = deltas_all.T

    def update(running):
        scores = (
            jnp.einsum("qhd,kd->hqk", q_piece, key_own, preferred_element_type=jnp.float32)
            * score_scale
        )
        scores = jnp.where(fold_visible[None], scores, masked_fill)
        prob_weights = jnp.where(fold_visible[None], jnp.exp(scores - stat_piece[:, :, None]), 0.0)
        grad_probs = jnp.einsum(
            "qhd,kd->hqk", g_piece, value_own, preferred_element_type=jnp.float32
        )
        grad_scores = (prob_weights * (grad_probs - delta_piece[:, :, None])).astype(jnp.bfloat16)
        grad_key = (
            jnp.einsum("hqk,qhd->kd", grad_scores, q_piece, preferred_element_type=jnp.float32)
            * score_scale
        )
        grad_value = jnp.einsum(
            "hqk,qhd->kd",
            prob_weights.astype(jnp.bfloat16),
            g_piece,
            preferred_element_type=jnp.float32,
        )
        return (grad_key, grad_value)

    grad_key_own, grad_value_own = update((zero_block, zero_block))
    empty_rows = jnp.zeros((row_count, keys_in.shape[1]), jnp.float32)
    placed_key = lax.dynamic_update_slice_in_dim(
        empty_rows, grad_key_own, key_value_group * HEAD_WIDTH, 1
    )
    placed_value = lax.dynamic_update_slice_in_dim(
        empty_rows, grad_value_own, key_value_group * HEAD_WIDTH, 1
    )
    key_gradient_rows, value_gradient_rows = (
        lax.psum_scatter(
            placed_key.astype(jnp.bfloat16), "ffn", scatter_dimension=0, tiled=True
        ).astype(jnp.float32),
        lax.psum_scatter(
            placed_value.astype(jnp.bfloat16), "ffn", scatter_dimension=0, tiled=True
        ).astype(jnp.float32),
    )
    row_terms = (row_contract(normed_rows, grad_gate), row_contract(normed_rows, grad_up))
    grad_w_gate, grad_w_up = (
        lax.psum_scatter(
            row_terms[0].astype(jnp.bfloat16), "ctx", scatter_dimension=0, tiled=True
        ).astype(jnp.float32),
        lax.psum_scatter(
            row_terms[1].astype(jnp.bfloat16), "ctx", scatter_dimension=0, tiled=True
        ).astype(jnp.float32),
    )
    col_terms = (row_contract(attended_rows, grad_rows), row_contract(activated, cot_rows))
    grad_w_out, grad_w_down = (
        lax.psum_scatter(
            col_terms[0].astype(jnp.bfloat16), "ctx", scatter_dimension=1, tiled=True
        ).astype(jnp.float32),
        lax.psum_scatter(
            col_terms[1].astype(jnp.bfloat16), "ctx", scatter_dimension=1, tiled=True
        ).astype(jnp.float32),
    )
    grad_queries = grad_query.reshape(row_count, resident_heads * HEAD_WIDTH).astype(jnp.bfloat16)
    return (
        mixed,
        grad_resid,
        grad_queries,
        key_gradient_rows,
        value_gradient_rows,
        grad_gain,
        grad_w_out,
        grad_w_gate,
        grad_w_up,
        grad_w_down,
    )


def solution(mesh):
    return jax.shard_map(
        body,
        mesh=mesh,
        in_specs=(
            P(("ctx", "ffn"), None),
            P("ctx", "ffn"),
            P("ctx", None),
            P("ctx", None),
            P("ffn", None),
            P(),
            P(None, "ffn"),
            P(None, "ffn"),
            P("ffn", None),
            P(("ctx", "ffn"), None),
            P("ctx"),
            P(),
        ),
        out_specs=(
            P(("ctx", "ffn"), None),
            P(("ctx", "ffn"), None),
            P("ctx", "ffn"),
            P(("ctx", "ffn"), None),
            P(("ctx", "ffn"), None),
            P(),
            P("ffn", "ctx"),
            P("ctx", "ffn"),
            P("ctx", "ffn"),
            P("ffn", "ctx"),
        ),
        check_vma=False,
    )
```

profile of v0, /device:TPU:1, one launch (start us, length us, event | category | flops | bytes accessed | tf_op | source)
XLA Modules:
  0.0 940.3 jit_solution(1435505484392055501)
XLA Ops:
  9.0 16.1 %all-gather = s32[8,1,128]{2,1,0:T(1,128)S(1)} all-gather(s32[1,1,128]{2,1,0:T(1,128)} %bitcast.186), channel_id=1, replica_groups=mesh['ctx'=8,'ffn'=16] {'ctx'}, dimensions={0}, use_global_device_ids=true | all-gather | bytes 4608 | tf_op jit(solution)/shard_map/all_gather | solution.py:67
  26.7 5.7 gather_fusion
  36.3 41.5 %while.21 = (s32[]{:T(128)}, f32[2,128]{1,0:T(2,128)S(1)}, f32[2,128]{1,0:T(2,128)S(1)}, f32[2,128,128]{2,1,0:T(8,128)S(1)}, bf16[128,2,128]{2,0,1:T(8,128)(2,1)...) while((s32[]{:T(128)}, f32[2,128]{1,0:T(2,128)S(1)}, ...), condition=%wide.region_5.6_spmd, body=%wide.region_2.5_spmd.sunk | while | flops 17187348 | bytes 1266056 | solution.py:104
  36.5 5.0 collective-permute-done
  42.4 4.9 collective-permute-done
  48.2 5.7 collective-permute-done
  60.7 4.9 collective-permute-done
  79.6 76.6 %reduce-scatter.10.cloned.1.call-done = bf16[8,4096]{1,0:T(8,128)(2,1)} async-done(((bf16[128,4096]{1,0:T(8,128)(2,1)}), bf16[8,4096]{1,0:T(8,128)(2,1)}) %reduce-scatter.10.cloned.1.call-update) | async-done | bytes 65552 | tf_op jit(solution)/shard_map/reduce_scatter | solution.py:112
  159.2 46.1 %all-gather.5.cloned.1.call-done = bf16[128,4096]{1,0:T(8,128)(2,1)} async-done(((bf16[8,4096]{1,0:T(8,128)(2,1)}), bf16[128,4096]{1,0:T(8,128)(2,1)}) %all-gather.5.cloned.1.call-update) | async-done | bytes 1048592 | tf_op jit(solution)/shard_map/all_gather | solution.py:122
  211.4 40.0 %all-gather.7.cloned.1.call-done = bf16[128,4096]{1,0:T(8,128)(2,1)} async-done(((bf16[8,4096]{1,0:T(8,128)(2,1)}), bf16[128,4096]{1,0:T(8,128)(2,1)}) %all-gather.7.cloned.1.call-update) | async-done | bytes 1048592 | tf_op jit(solution)/shard_map/all_gather | solution.py:136
  263.6 59.9 %reduce-scatter.14.cloned.1.call-done = bf16[8,4096]{1,0:T(8,128)(2,1)} async-done(((bf16[128,4096]{1,0:T(8,128)(2,1)}), bf16[8,4096]{1,0:T(8,128)(2,1)}) %reduce-scatter.14.cloned.1.call-update) | async-done | bytes 65552 | tf_op jit(solution)/shard_map/reduce_scatter | solution.py:142
  325.6 67.8 %reduce-scatter.12.cloned.1.call-done = bf16[8,4096]{1,0:T(8,128)(2,1)} async-done(((bf16[128,4096]{1,0:T(8,128)(2,1)}), bf16[8,4096]{1,0:T(8,128)(2,1)}) %reduce-scatter.12.cloned.1.call-update) | async-done | bytes 65552 | tf_op jit(solution)/shard_map/reduce_scatter | solution.py:129
  395.1 14.5 %all_gather.33 = f32[1024,2]{0,1:T(2,128)S(1)} all-gather(f32[128,2]{0,1:T(2,128)S(1)} %bitcast.190), channel_id=1, replica_groups=mesh['ctx'=8,'ffn'=16] {'ctx'}, dimensions={0}, use_global_device_ids=true | all-gather | bytes 9216 | tf_op jit(solution)/shard_map/all_gather | solution.py:171
  410.5 20.7 %all_gather.32 = bf16[1024,256]{0,1:T(8,128)(2,1)S(1)} all-gather(bf16[128,256]{0,1:T(8,128)(2,1)S(1)} %copy.44), channel_id=1, replica_groups=mesh['ctx'=8,'ffn'=16] {'ctx'}, dimensions={0}, use_global_device_ids=true | all-gather | bytes 589824 | tf_op jit(solution)/shard_map/all_gather | solution.py:198
  434.2 9.5 %all-gather.9.cloned.1.call-done = bf16[128,4096]{1,0:T(8,128)(2,1)} async-done(((bf16[8,4096]{1,0:T(8,128)(2,1)}), bf16[128,4096]{1,0:T(8,128)(2,1)}) %all-gather.9.cloned.1.call-update) | async-done | bytes 1048592 | tf_op jit(solution)/shard_map/all_gather | solution.py:159
  445.9 24.8 %all_gather.34 = bf16[1024,256]{1,0:T(8,128)(2,1)} all-gather(bf16[128,256]{1,0:T(8,128)(2,1)S(1)} %convolution_convert_fusion.6), channel_id=1, replica_groups=mesh['ctx'=8,'ffn'=16] {'ctx'}, dimensions={0}, use_global_device_ids=true | all-gather | bytes 589824 | tf_op jit(solution)/shard_map/all_gather | solution.py:199
  470.8 14.9 %all_gather.35 = f32[1024,2]{0,1:T(2,128)S(1)} all-gather(f32[128,2]{0,1:T(2,128)S(1)} %multiply_reduce_fusion), channel_id=1, replica_groups=mesh['ctx'=8,'ffn'=16] {'ctx'}, dimensions={0}, use_global_device_ids=true | all-gather | bytes 9216 | tf_op jit(solution)/shard_map/all_gather | solution.py:172
  507.7 23.3 %all_gather.30 = bf16[1024,2,128]{2,0,1:T(8,128)(2,1)S(1)} all-gather(bf16[128,2,128]{2,0,1:T(8,128)(2,1)S(1)} %copy-done.17), channel_id=1, replica_groups=mesh['ctx'=8,'ffn'=16] {'ctx'}, dimensions={0}, use_global_device_ids=true | all-gather | bytes 589824 | tf_op jit(solution)/shard_map/all_gather | solution.py:174
  533.0 77.0 %psum.7 = f32[4096]{0:T(1024)} all-reduce(f32[4096]{0:T(1024)S(1)} %copy-done.21), channel_id=1, replica_groups=mesh['ctx'=8,'ffn'=16] {'ctx','ffn'}, use_global_device_ids=true, to_apply=%region_15.16 | all-reduce | flops 4096 | bytes 32768 | tf_op jit(solution)/shard_map/psum | solution.py:158
  613.9 13.0 %reduce-scatter.18.cloned.1.call-done = bf16[8,1024]{1,0:T(8,128)(2,1)} async-done(((bf16[128,1024]{1,0:T(8,128)(2,1)}), bf16[8,1024]{1,0:T(8,128)(2,1)}) %reduce-scatter.18.cloned.1.call-update) | async-done | bytes 16400 | tf_op jit(solution)/shard_map/reduce_scatter | solution.py:243
  628.2 82.1 %reduce-scatter.22.cloned.1.call-done = bf16[512,448]{0,1:T(8,128)(2,1)} async-done(((bf16[4096,448]{0,1:T(8,128)(2,1)}), bf16[512,448]{0,1:T(8,128)(2,1)}) %reduce-scatter.22.cloned.1.call-update) | async-done | bytes 458768 | tf_op jit(solution)/shard_map/reduce_scatter | solution.py:249
  712.4 81.6 %reduce-scatter.24.cloned.1.call-done = bf16[512,448]{0,1:T(8,128)(2,1)} async-done(((bf16[4096,448]{0,1:T(8,128)(2,1)}), bf16[512,448]{0,1:T(8,128)(2,1)}) %reduce-scatter.24.cloned.1.call-update) | async-done | bytes 458768 | tf_op jit(solution)/shard_map/reduce_scatter | solution.py:252
  796.0 81.8 %reduce-scatter.26.cloned.1.call-done = bf16[448,512]{1,0:T(8,128)(2,1)} async-done(((bf16[448,4096]{1,0:T(8,128)(2,1)}), bf16[448,512]{1,0:T(8,128)(2,1)}) %reduce-scatter.26.cloned.1.call-update) | async-done | bytes 458768 | tf_op jit(solution)/shard_map/reduce_scatter | solution.py:261
  879.9 51.8 %reduce-scatter.20.cloned.1.call-done = bf16[256,512]{1,0:T(8,128)(2,1)} async-done(((bf16[256,4096]{1,0:T(8,128)(2,1)}), bf16[256,512]{1,0:T(8,128)(2,1)}) %reduce-scatter.20.cloned.1.call-update) | async-done | bytes 262160 | tf_op jit(solution)/shard_map/reduce_scatter | solution.py:258
  (220 shorter events, 97.4 us)
Async XLA Ops:
  7.2 148.9 %reduce-scatter.10.cloned.1.call-start = ((), (), s32[]{:S(2)}) async-start(), calls=%async_computation.9 | async-start | bytes 1114112 | tf_op jit(solution)/shard_map/reduce_scatter | solution.py:112
  36.3 5.2 collective-permute-start
  42.0 5.3 collective-permute-start
  47.9 6.1 collective-permute-start
  54.5 5.3 collective-permute-start
  60.3 5.3 collective-permute-start
  66.1 5.3 collective-permute-start
  72.0 5.3 collective-permute-start
  77.8 81.3 %copy-start.24 = (s32[128]{0:T(128)}, s32[128]{0:T(128)S(1)}, u32[]{:S(2)}) copy-start(s32[128]{0:T(128)S(1)} %get-tuple-element.564) | copy-start | bytes 1540
  77.8 81.3 %copy-start.25 = (s32[1024]{0:T(1024)}, s32[1024]{0:T(1024)S(1)}, u32[]{:S(2)}) copy-start(s32[1024]{0:T(1024)S(1)} %get-tuple-element.565) | copy-start | bytes 12292
  77.8 331.8 %copy-start.22 = (s32[1024]{0:T(1024)}, s32[1024]{0:T(1024)S(1)}, u32[]{:S(2)}) copy-start(s32[1024]{0:T(1024)S(1)} %get-tuple-element.561) | copy-start | bytes 12292
  79.5 125.8 %all-gather.5.cloned.1.call-start = ((), (), s32[]{:S(2)}) async-start(), calls=%async_computation.10 | async-start | bytes 1114112 | tf_op jit(solution)/shard_map/all_gather | solution.py:122
  158.4 93.0 %all-gather.7.cloned.1.call-start = ((), (), s32[]{:S(2)}) async-start(), calls=%async_computation.12 | async-start | bytes 1114112 | tf_op jit(solution)/shard_map/all_gather | solution.py:136
  159.1 164.4 %reduce-scatter.14.cloned.1.call-start = ((), (), s32[]{:S(2)}) async-start(), calls=%async_computation.13 | async-start | bytes 1114112 | tf_op jit(solution)/shard_map/reduce_scatter | solution.py:142
  259.6 133.7 %copy-start.18 = (bf16[8,4096]{1,0:T(8,128)(2,1)S(1)}, bf16[8,4096]{1,0:T(8,128)(2,1)}, u32[]{:S(2)}) copy-start(bf16[8,4096]{1,0:T(8,128)(2,1)} %param.23) | copy-start | bytes 196612
  259.6 133.7 %reduce-scatter.12.cloned.1.call-start = ((), (), s32[]{:S(2)}) async-start(), calls=%async_computation.11 | async-start | bytes 1114112 | tf_op jit(solution)/shard_map/reduce_scatter | solution.py:129
  263.5 180.2 %all-gather.9.cloned.1.call-start = ((), (), s32[]{:S(2)}) async-start(), calls=%async_computation.14 | async-start | bytes 1114112 | tf_op jit(solution)/shard_map/all_gather | solution.py:159
  395.0 217.5 %reduce-scatter.16.cloned.1.call-start = ((), (), s32[]{:S(2)}) async-start(), calls=%async_computation.15 | async-start | bytes 278528 | tf_op jit(solution)/shard_map/reduce_scatter | solution.py:240
  488.6 138.3 %reduce-scatter.18.cloned.1.call-start = ((), (), s32[]{:S(2)}) async-start(), calls=%async_computation.16 | async-start | bytes 278528 | tf_op jit(solution)/shard_map/reduce_scatter | solution.py:243
  491.1 219.2 %reduce-scatter.22.cloned.1.call-start = ((), (), s32[]{:S(2)}) async-start(), calls=%async_computation.18 | async-start | bytes 4128768 | tf_op jit(solution)/shard_map/reduce_scatter | solution.py:249
  495.1 298.8 %reduce-scatter.24.cloned.1.call-start = ((), (), s32[]{:S(2)}) async-start(), calls=%async_computation.19 | async-start | bytes 4128768 | tf_op jit(solution)/shard_map/reduce_scatter | solution.py:252
  499.0 378.8 %reduce-scatter.26.cloned.1.call-start = ((), (), s32[]{:S(2)}) async-start(), calls=%async_computation.20 | async-start | bytes 4128768 | tf_op jit(solution)/shard_map/reduce_scatter | solution.py:261
  503.3 106.7 %copy-start.15 = (bf16[128,256]{0,1:T(8,128)(2,1)S(1)}, bf16[128,256]{0,1:T(8,128)(2,1)}, u32[]{:S(2)}) copy-start(bf16[128,256]{0,1:T(8,128)(2,1)} %copy-done.14) | copy-start | bytes 196612
  503.3 428.3 %reduce-scatter.20.cloned.1.call-start = ((), (), s32[]{:S(2)}) async-start(), calls=%async_computation.17 | async-start | bytes 2359296 | tf_op jit(solution)/shard_map/reduce_scatter | solution.py:258
  (24 other events, 469.8 us)
Sparse Core Ops, SparseCore 0:
  79.6 76.4 reduce-scatter.9
  159.2 46.0 all-gather.4
  207.7 43.6 all-gather.6
  259.7 63.7 reduce-scatter.13
  327.1 66.1 reduce-scatter.11
  396.2 47.4 all-gather.8
  488.7 69.1 reduce-scatter.15
  562.2 64.6 reduce-scatter.17
  629.3 80.9 reduce-scatter.21
  712.6 81.3 reduce-scatter.23
  796.4 81.3 reduce-scatter.25
  880.1 51.4 reduce-scatter.19
where the time goes:
time: 943 us; the launch traced here: 940 us
  waiting for transfers between devices  646 us (69%)
  blocking collectives  191 us (20%)
  matrix products  46.8 us (5%)
  other arithmetic  20.6 us (2%)
  local copies, waits for them, and re-layouts  18.9 us (2%)
  between operations  14.6 us (2%)
    reduce_scatter x1, waiting for transfers between devices, body(): lax.psum_scatter(row_terms[0].astype(jnp.bfloat16), 'ctx', scatter_dimens...  82.1 us
    reduce_scatter x1, waiting for transfers between devices, body(): lax.psum_scatter(col_terms[1].astype(jnp.bfloat16), 'ctx', scatter_dimens...  81.8 us
    reduce_scatter x1, waiting for transfers between devices, body(): lax.psum_scatter(row_terms[1].astype(jnp.bfloat16), 'ctx', scatter_dimens...  81.6 us
    psum x1, blocking collectives, body(): lax.psum(jnp.sum(grad_normed * hidden_f * inv_rms, axis=0), ('ctx', 'ffn'))  77 us
    reduce_scatter x1, waiting for transfers between devices, body(): lax.psum_scatter(jnp.dot(attended_rows, w_out, preferred_element_type=jnp...  76.6 us
    reduce_scatter x1, waiting for transfers between devices, body(): lax.psum_scatter(jnp.dot(activated, w_down, preferred_element_type=jnp.fl...  67.8 us
    reduce_scatter x1, waiting for transfers between devices, body(): lax.psum_scatter((jnp.dot(grad_gate, w_gate.T, preferred_element_type=jnp...  59.9 us
    reduce_scatter x1, waiting for transfers between devices, body(): lax.psum_scatter(col_terms[0].astype(jnp.bfloat16), 'ctx', scatter_dimens...  51.8 us
  transfers between devices with their start and end apart: 19, of which 18 were waited for; matrix products, arithmetic and copies ran while one was open for 5% of the time, Pallas kernels for 0%

commit v1 on v0

v1 whole, which is shorter than its diff:
```python
import functools
import math

import jax
import jax.numpy as jnp
from jax import lax
from jax.experimental import pallas as pl
from jax.experimental.pallas import tpu as pltpu
from jax.sharding import PartitionSpec as P

MESH = pl.DeviceIdType.MESH
F32 = jnp.float32
BF = jnp.bfloat16
CTX = 8
CHIPS = 8
HW = 128
SCALE = 1.0 / math.sqrt(128)
NEG = -1e30
EPS = 1e-05
NT = (((1,), (1,)), ((), ()))


class Net:
    def __init__(self, ssem, rsem):
        self.ssem, self.rsem, self.used = ssem, rsem, 0
        self.c = lax.axis_index("ctx")
        self.f = lax.axis_index("ffn")
        self.core = lax.rem(self.f, 2)
        self.chip = self.f // 2
        self.partner = self.f + 1 - 2 * self.core

    def copy(self, src, dst, c=None, f=None):
        n = self.used
        self.used = n + 1
        return pltpu.make_async_remote_copy(
            src_ref=src,
            dst_ref=dst,
            send_sem=self.ssem.at[n],
            recv_sem=self.rsem.at[n],
            device_id=(self.c if c is None else c, self.f if f is None else f),
            device_id_type=MESH,
        )

    def ctx_to(self, k):
        return lax.rem(self.c + k, CTX)

    def ctx_from(self, k):
        return lax.rem(self.c + CTX - k, CTX)

    def chip_to(self, k):
        return lax.rem(self.chip + k, CHIPS)

    def chip_from(self, k):
        return lax.rem(self.chip + CHIPS - k, CHIPS)

    def greet(self, all_ffn):
        barrier = pltpu.get_barrier_semaphore()
        count = 0
        for k in range(1, CTX):
            pl.semaphore_signal(
                barrier, inc=1, device_id=(self.ctx_to(k), self.f), device_id_type=MESH
            )
            count += 1
        if all_ffn:
            for k in range(1, 16):
                pl.semaphore_signal(
                    barrier,
                    inc=1,
                    device_id=(self.c, lax.rem(self.f + k, 16)),
                    device_id_type=MESH,
                )
                count += 1
        else:
            for k in range(1, CHIPS):
                pl.semaphore_signal(
                    barrier,
                    inc=1,
                    device_id=(self.c, self.chip_to(k) * 2 + self.core),
                    device_id_type=MESH,
                )
                count += 1
            pl.semaphore_signal(
                barrier, inc=1, device_id=(self.c, self.partner), device_id_type=MESH
            )
            count += 1
        pl.semaphore_wait(barrier, count)


def ctx_gather(net, src, dst):
    return [net.copy(src, dst.at[net.c], c=net.ctx_to(k)) for k in range(1, CTX)]


def ctx_columns(net, src, dst):
    out = []
    for k in range(1, CTX):
        to = net.ctx_to(k)
        cols = pl.ds(pl.multiple_of(to * 512, 512), 512)
        out.append(net.copy(src.at[:, :, cols], dst.at[net.c], c=to))
    return out


class FfnGather:
    def __init__(self, net, src, dst):
        self.net, self.dst = net, dst
        self.far = [
            net.copy(src, dst.at[net.f], f=net.chip_to(k) * 2 + net.core) for k in range(1, CHIPS)
        ]
        self.near = [net.copy(src, dst.at[net.f], f=net.partner)]

    def start(self):
        for cp in self.far:
            cp.start()
        self.near[0].start()

    def forward(self):
        net = self.net
        for k in range(1, CHIPS):
            self.far[k - 1].wait_recv()
            block = self.dst.at[net.chip_from(k) * 2 + net.core]
            cp = net.copy(block, block, f=net.partner)
            cp.start()
            self.near.append(cp)

    def finish(self):
        for cp in self.near:
            cp.wait_recv()

    def drain(self):
        for cp in self.far + self.near:
            cp.wait_send()


class FfnScatter:
    def __init__(self, net, part, pair_in, summed, got):
        self.net, self.part, self.pair_in, self.summed, self.got = net, part, pair_in, summed, got
        self.pair = net.copy(part.at[:, 1 - net.core], pair_in, f=net.partner)
        self.far = [
            net.copy(
                summed.at[net.chip_to(k)],
                got.at[net.chip],
                f=net.chip_to(k) * 2 + net.core,
            )
            for k in range(1, CHIPS)
        ]

    def start(self):
        self.pair.start()

    def chip_sum(self, to):
        return self.part[to, self.net.core].astype(F32) + self.pair_in[to].astype(F32)

    def middle(self):
        net = self.net
        self.pair.wait_recv()
        for k in range(1, CHIPS):
            to = net.chip_to(k)
            self.summed[to] = self.chip_sum(to).astype(BF)
            self.far[k - 1].start()

    def finish(self):
        net = self.net
        total = self.chip_sum(net.chip)
        for k in range(1, CHIPS):
            self.far[k - 1].wait_recv()
            total = total + self.got[net.chip_from(k)].astype(F32)
        return total

    def drain(self):
        self.pair.wait_send()
        for cp in self.far:
            cp.wait_send()


def seg_starts(doc_ref, pos):
    doc = doc_ref[...]
    start = jnp.zeros_like(pos)
    for v in (1, 2, 3):
        edge = jnp.sum((doc < v).astype(F32))
        start = jnp.where(pos >= edge, jnp.maximum(start, edge), start)
    return start


def as_column(row):
    return jnp.transpose(jnp.broadcast_to(row, (128, 128)))


def as_row(column):
    return jnp.transpose(jnp.broadcast_to(column, (128, 128)))[0:1, :]


def front(
    keys, values, q, pos, doc, wout, resid, gain, cot,
    att, lse, k_all, v_all, q_all, pos_all, hid, inv, nrm_all, cot_all,
    part, pair_in, summed, got, nbuf, ssem, rsem,
):
    net = Net(ssem, rsem)
    c, f = net.c, net.f
    net.greet(False)
    cols = pl.ds(pl.multiple_of(net.chip * 128, 128), 128)
    first = (
        ctx_gather(net, keys.at[:, cols], k_all)
        + ctx_gather(net, values.at[:, cols], v_all)
        + ctx_gather(net, pos, pos_all)
    )
    for cp in first:
        cp.start()
    k_all[c] = keys[:, cols]
    v_all[c] = values[:, cols]
    pos_all[c] = pos[...]
    q_all[c] = q[...]
    cot_all[f] = cot[...]
    cot_gather = FfnGather(net, cot, cot_all)
    q_gather = ctx_gather(net, q, q_all)
    for cp in first:
        cp.wait_recv()
    cot_gather.start()
    for cp in q_gather:
        cp.start()
    kpos = jnp.concatenate([pos_all[i] for i in range(CTX)], axis=1)
    qpos = as_column(pos[...])[:, 0:1]
    qstart = seg_starts(doc, qpos)
    visible = (kpos <= qpos) & (kpos >= qstart)
    k = k_all[...].reshape(1024, 128)
    v = v_all[...].reshape(1024, 128)
    rows = []
    for h in range(2):
        qh = q[:, h * 128 : (h + 1) * 128]
        s = lax.dot_general(qh, k, NT, preferred_element_type=F32) * SCALE
        s = jnp.where(visible, s, NEG)
        top = jnp.max(s, axis=1, keepdims=True)
        w = jnp.where(visible, jnp.exp(s - top), 0.0)
        total = jnp.sum(w, axis=1, keepdims=True)
        o = jnp.dot(w.astype(BF), v, preferred_element_type=F32) / total
        att[:, h * 128 : (h + 1) * 128] = o.astype(BF)
        rows.append(as_row(top + jnp.log(total)))
    lse[...] = jnp.concatenate(rows + [jnp.zeros((6, 128), F32)], axis=0)
    a = att[...]
    for n in range(8):
        span = slice(n * 512, (n + 1) * 512)
        r = jnp.dot(a, wout[:, span], preferred_element_type=F32)
        for b in range(16):
            part[b // 2, b % 2, :, span] = r[b * 8 : (b + 1) * 8].astype(BF)
    rs = FfnScatter(net, part, pair_in, summed, got)
    rs.start()
    rs.middle()
    cot_gather.forward()
    projected = rs.finish()
    hidden = (resid[...].astype(F32) + projected).astype(BF)
    hid[...] = hidden
    hf = hidden.astype(F32)
    ir = lax.rsqrt(jnp.mean(hf * hf, axis=1, keepdims=True) + EPS)
    inv[...] = jnp.broadcast_to(ir, (8, 128))
    normed = (hf * ir * gain[...]).astype(BF)
    nbuf[...] = normed
    nrm_all[f] = normed
    ag = FfnGather(net, nbuf, nrm_all)
    ag.start()
    cot_gather.finish()
    ag.forward()
    ag.finish()
    for cp in q_gather:
        cp.wait_recv()
    for cp in first + q_gather:
        cp.wait_send()
    cot_gather.drain()
    rs.drain()
    ag.drain()


def back(
    gn, mx, hid, inv, cot, gain, nrm_all, cot_all, gu, act, att, wout, q, q_all, k_all, v_all,
    pos_all, doc, lse,
    mixed, gres, dq, kg, vg, gg, nrm_c, cot_c, gres_c, gu_all, act_all, att_all,
    pair_in, summed, got, pair_in2, summed2, got2, gbuf, grows, ga, ga_all, stats, stats_all,
    kv, kv_in, gsum, gpair, gchip, gctx_b, gctx, ssem, rsem,
):
    net = Net(ssem, rsem)
    c, f = net.c, net.f
    net.greet(True)
    rs = FfnScatter(net, gn, pair_in, summed, got)
    rs2 = FfnScatter(net, mx, pair_in2, summed2, got2)
    rs.start()
    rs2.start()
    rs.middle()
    bulk = (
        ctx_gather(net, att, att_all)
        + ctx_gather(net, gu, gu_all)
        + ctx_gather(net, act, act_all)
        + ctx_columns(net, nrm_all, nrm_c)
        + ctx_columns(net, cot_all, cot_c)
    )
    for cp in bulk:
        cp.start()
    own = pl.ds(pl.multiple_of(c * 512, 512), 512)
    att_all[c] = att[...]
    gu_all[c] = gu[...]
    act_all[c] = act[...]
    nrm_c[c] = nrm_all[:, :, own]
    cot_c[c] = cot_all[:, :, own]
    gnorm = rs.finish()
    hf = hid[...].astype(F32)
    ir = inv[:, 0:1]
    gained = gnorm * gain[...]
    cube = ir * ir * ir
    mean = jnp.mean(gained * hf, axis=1, keepdims=True)
    gr = (cot[...].astype(F32) + ir * gained - hf * cube * mean).astype(BF)
    gres[...] = gr
    gbuf[...] = gr
    grows[f] = gr
    gsum[...] = jnp.sum(gnorm * hf * ir, axis=0, keepdims=True)
    ag = FfnGather(net, gbuf, grows)
    ag.start()
    g1 = net.copy(gsum, gpair, f=net.partner)
    g1.start()
    rs2.middle()
    g1.wait_recv()
    gchip[net.chip] = gsum[...] + gpair[...]
    g2 = [
        net.copy(gchip.at[net.chip], gchip.at[net.chip], f=net.chip_to(k_) * 2 + net.core)
        for k_ in range(1, CHIPS)
    ]
    for cp in g2:
        cp.start()
    ag.forward()
    ag.finish()
    rows = jnp.concatenate([grows[b] for b in range(16)], axis=0)
    gat = lax.dot_general(rows, wout[...], NT, preferred_element_type=F32).astype(BF)
    ga[...] = gat
    ga_all[c] = gat
    prod = gat.astype(F32) * att[...].astype(F32)
    delta = [jnp.sum(prod[:, h * 128 : (h + 1) * 128], axis=1, keepdims=True) for h in range(2)]
    st = jnp.concatenate(
        [lse[0:2, :], as_row(delta[0]), as_row(delta[1]), jnp.zeros((4, 128), F32)], axis=0
    )
    stats[...] = st
    stats_all[c] = st
    late = ctx_gather(net, ga, ga_all) + ctx_gather(net, stats, stats_all)
    for cp in late:
        cp.start()
    late2 = ctx_columns(net, grows, gres_c)
    for cp in late2:
        cp.start()
    gres_c[c] = grows[:, :, own]
    kpos = jnp.concatenate([pos_all[i] for i in range(CTX)], axis=1)
    mypos = pos_all[c]
    qpos = as_column(mypos)[:, 0:1]
    visible = (kpos <= qpos) & (kpos >= seg_starts(doc, qpos))
    k = k_all[...].reshape(1024, 128)
    v = v_all[...].reshape(1024, 128)
    for h in range(2):
        hs = slice(h * 128, (h + 1) * 128)
        s = lax.dot_general(q[:, hs], k, NT, preferred_element_type=F32) * SCALE
        lcol = as_column(lse[h : h + 1, :])[:, 0:1]
        p = jnp.where(visible, jnp.exp(jnp.where(visible, s, NEG) - lcol), 0.0)
        dp = lax.dot_general(gat[:, hs], v, NT, preferred_element_type=F32)
        ds = (p * (dp - delta[h])).astype(BF)
        dq[:, hs] = (jnp.dot(ds, k, preferred_element_type=F32) * SCALE).astype(BF)
    for cp in g2:
        cp.wait_recv()
    tot = gchip[0]
    for i in range(1, CHIPS):
        tot = tot + gchip[i]
    gctx_b[...] = tot
    gctx[c] = tot
    g3 = ctx_gather(net, gctx_b, gctx)
    for cp in g3:
        cp.start()
    mixed[...] = (hf + rs2.finish()).astype(BF)
    for cp in late:
        cp.wait_recv()
    qrow = kpos
    qs = seg_starts(doc, kpos)
    vis_t = (qpos <= qrow) & (qpos >= qs)
    k_own = k_all[c]
    v_own = v_all[c]
    dk = jnp.zeros((128, 128), F32)
    dv = jnp.zeros((128, 128), F32)
    for h in range(2):
        hs = slice(h * 128, (h + 1) * 128)
        qa = q_all[:, :, hs].reshape(1024, 128)
        gaa = ga_all[:, :, hs].reshape(1024, 128)
        lrow = jnp.concatenate([stats_all[i, h : h + 1, :] for i in range(CTX)], axis=1)
        drow = jnp.concatenate([stats_all[i, 2 + h : 3 + h, :] for i in range(CTX)], axis=1)
        s = lax.dot_general(k_own, qa, NT, preferred_element_type=F32) * SCALE
        p = jnp.where(vis_t, jnp.exp(jnp.where(vis_t, s, NEG) - lrow), 0.0)
        dp = lax.dot_general(v_own, gaa, NT, preferred_element_type=F32)
        ds = (p * (dp - drow)).astype(BF)
        dk = dk + jnp.dot(ds, qa, preferred_element_type=F32)
        dv = dv + jnp.dot(p.astype(BF), gaa, preferred_element_type=F32)
    dkv = jnp.concatenate([dk * SCALE, dv], axis=1)
    for b in range(16):
        kv[b] = dkv[b * 8 : (b + 1) * 8]
    kv_in[f] = kv[f]
    last = []
    for n in range(1, 16):
        to = lax.rem(f + n, 16)
        last.append(net.copy(kv.at[to], kv_in.at[f], f=to))
    for cp in last:
        cp.start()
    for cp in g3:
        cp.wait_recv()
    tot = gctx[0]
    for i in range(1, CTX):
        tot = tot + gctx[i]
    gg[...] = tot
    for cp in last:
        cp.wait_recv()
    for g in range(8):
        pair = kv_in[2 * g] + kv_in[2 * g + 1]
        kg[:, g * 128 : (g + 1) * 128] = pair[:, 0:128]
        vg[:, g * 128 : (g + 1) * 128] = pair[:, 128:256]
    for cp in bulk + late2:
        cp.wait_recv()
    for cp in bulk + late + late2 + g2 + g3 + last + [g1]:
        cp.wait_send()
    rs.drain()
    rs2.drain()
    ag.drain()


VM = pl.BlockSpec(memory_space=pltpu.VMEM)


def call(kernel, outs, scratch, sems, collective_id, args):
    return pl.pallas_call(
        kernel,
        out_shape=[jax.ShapeDtypeStruct(s, d) for s, d in outs],
        in_specs=[VM] * len(args),
        out_specs=[VM] * len(outs),
        scratch_shapes=[pltpu.VMEM(s, d) for s, d in scratch]
        + [pltpu.SemaphoreType.DMA((sems,)), pltpu.SemaphoreType.DMA((sems,))],
        compiler_params=pltpu.CompilerParams(
            collective_id=collective_id, has_side_effects=True, vmem_limit_bytes=60 * 2**20
        ),
    )(*args)


def body(
    resid_in, queries, keys_in, value_rows_input, w_out, norm_gain, w_gate, w_up, w_down,
    cotangent, positions, doc_ids,
):
    pos = positions.astype(F32).reshape(1, 128)
    doc = doc_ids.reshape(8, 128)
    gain = norm_gain.reshape(1, 4096)
    att, lse, k_all, v_all, q_all, pos_all, hid, inv, nrm_all, cot_all = call(
        front,
        [
            ((128, 256), BF),
            ((8, 128), F32),
            ((8, 128, 128), BF),
            ((8, 128, 128), BF),
            ((8, 128, 256), BF),
            ((8, 1, 128), F32),
            ((8, 4096), BF),
            ((8, 128), F32),
            ((16, 8, 4096), BF),
            ((16, 8, 4096), BF),
        ],
        [
            ((8, 2, 8, 4096), BF),
            ((8, 8, 4096), BF),
            ((8, 8, 4096), BF),
            ((8, 8, 4096), BF),
            ((8, 4096), BF),
        ],
        80,
        0,
        (keys_in, value_rows_input, queries, pos, doc, w_out, resid_in, gain, cotangent),
    )
    normed_rows = nrm_all.reshape(128, 4096)
    cot_rows = cot_all.reshape(128, 4096)
    gate_pre = jnp.dot(normed_rows, w_gate, preferred_element_type=F32)
    up_proj = jnp.dot(normed_rows, w_up, preferred_element_type=F32)
    sig = jax.nn.sigmoid(gate_pre)
    activated = (gate_pre * sig * up_proj).astype(BF)
    mx = jnp.dot(activated, w_down, preferred_element_type=F32).astype(BF)
    grad_act = jnp.dot(cot_rows, w_down.T, preferred_element_type=F32)
    grad_up = (grad_act * gate_pre * sig).astype(BF)
    grad_gate = (grad_act * up_proj * sig * (1.0 + gate_pre * (1.0 - sig))).astype(BF)
    gn = (
        jnp.dot(grad_gate, w_gate.T, preferred_element_type=F32)
        + jnp.dot(grad_up, w_up.T, preferred_element_type=F32)
    ).astype(BF)
    gu = jnp.concatenate([grad_gate, grad_up], axis=1)
    (mixed, gres, dq, kg, vg, gg, nrm_c, cot_c, gres_c, gu_all, act_all, att_all) = call(
        back,
        [
            ((8, 4096), BF),
            ((8, 4096), BF),
            ((128, 256), BF),
            ((8, 1024), F32),
            ((8, 1024), F32),
            ((1, 4096), F32),
            ((8, 16, 8, 512), BF),
            ((8, 16, 8, 512), BF),
            ((8, 16, 8, 512), BF),
            ((8, 128, 896), BF),
            ((8, 128, 448), BF),
            ((8, 128, 256), BF),
        ],
        [((8, 8, 4096), BF)] * 6
        + [
            ((8, 4096), BF),
            ((16, 8, 4096), BF),
            ((128, 256), BF),
            ((8, 128, 256), BF),
            ((8, 128), F32),
            ((8, 8, 128), F32),
            ((16, 8, 256), F32),
            ((16, 8, 256), F32),
            ((1, 4096), F32),
            ((1, 4096), F32),
            ((8, 1, 4096), F32),
            ((1, 4096), F32),
            ((8, 1, 4096), F32),
        ],
        140,
        1,
        (
            gn.reshape(8, 2, 8, 4096), mx.reshape(8, 2, 8, 4096), hid, inv, cotangent, gain,
            nrm_all, cot_all, gu, activated, att, w_out, queries, q_all, k_all, v_all,
            pos_all, doc, lse,
        ),
    )
    nrm_c = nrm_c.reshape(1024, 512)
    cot_c = cot_c.reshape(1024, 512)
    gres_c = gres_c.reshape(1024, 512)
    gu_all = gu_all.reshape(1024, 896)
    contract = functools.partial(
        lax.dot_general,
        dimension_numbers=(((0,), (0,)), ((), ())),
        preferred_element_type=F32,
    )
    grad_w_out = contract(att_all.reshape(1024, 256), gres_c)
    grad_w_gate = contract(nrm_c, gu_all[:, :448])
    grad_w_up = contract(nrm_c, gu_all[:, 448:])
    grad_w_down = contract(act_all.reshape(1024, 448), cot_c)
    return (
        mixed, gres, dq, kg, vg, gg.reshape(4096), grad_w_out, grad_w_gate, grad_w_up, grad_w_down,
    )


def solution(mesh):
    rows = P(("ctx", "ffn"), None)
    return jax.shard_map(
        body,
        mesh=mesh,
        in_specs=(
            rows, P("ctx", "ffn"), P("ctx", None), P("ctx", None), P("ffn", None), P(),
            P(None, "ffn"), P(None, "ffn"), P("ffn", None), rows, P("ctx"), P(),
        ),
        out_specs=(
            rows, rows, P("ctx", "ffn"), rows, rows, P(), P("ffn", "ctx"), P("ctx", "ffn"),
            P("ctx", "ffn"), P("ffn", "ctx"),
        ),
        check_vma=False,
    )
```

time: 943 us -> 199 us (0.21)
  waiting for transfers between devices: 646 us -> 0 us
  blocking collectives: 191 us -> 0 us
  Pallas kernels: 0 us -> 166 us
  matrix products: 46.8 us -> 24.3 us
  other arithmetic: 20.6 us -> 1.96 us
  between operations: 14.6 us -> 0.84 us
  local copies, waits for them, and re-layouts: 18.9 us -> 5.45 us
    reduce_scatter x9 -> x0, waiting for transfers between devices: 514 us -> none  [the longest x1 82.1 us: body(): lax.psum_scatter(row_terms[0].astype(jnp.bfloat16), 'ctx', scatter_dimens...]
    pallas_call x0 -> x2, Pallas kernels: none -> 166 us  [call(): pl.pallas_call(kernel, out_shape=[jax.ShapeDtypeStruct(s, d) for s, d in...]
    all_gather x6 -> x0, blocking collectives: 114 us -> none  [the longest x1 24.8 us: body(): lax.all_gather(grad_attended, 'ctx', axis=0, tiled=True)]
    all_gather x3 -> x0, waiting for transfers between devices: 95.6 us -> none  [the longest x1 46.1 us: body(): normed_rows = lax.all_gather(normed, 'ffn', axis=0, tiled=True)]
    psum x1 -> x0, blocking collectives: 77 us -> none  [body(): lax.psum(jnp.sum(grad_normed * hidden_f * inv_rms, axis=0), ('ctx', 'ffn'))]
    ppermute x7 -> x0, waiting for transfers between devices: 35.3 us -> none  [passed_along(): lax.ppermute(value, axis, [(i, (i + by) % count) for i in range(count)])]
    dot_general x33 -> x10, matrix products: 46.8 us -> 24.3 us  [the longest x1 3.8 us: body(): grad_w_up = contract(nrm_c, gu_all[:, 448:])]
    convert_element_type x10 -> x0, other arithmetic: 13.9 us -> none  [the longest x2 4.11 us: body(): grad_w_gate, grad_w_up = (lax.psum_scatter(row_terms[0].astype(jnp.bfloat...]
  transfers between devices with their start and end apart: 19 -> 0, of which waited for: 18 -> 0; matrix products, arithmetic and copies ran while one was open for 5% -> 0% of each run, Pallas kernels for 0% -> 0%
where the time goes in v1:
time: 199 us
  Pallas kernels  166 us (83%)
  matrix products  24.3 us (12%)
  local copies, waits for them, and re-layouts  5.45 us (3%)
    pallas_call x2, Pallas kernels, call(): pl.pallas_call(kernel, out_shape=[jax.ShapeDtypeStruct(s, d) for s, d in...  166 us
    unnamed x38, local copies, waits for them, and re-layouts  5.06 us

profile of v1, /device:TPU:1, one launch (start us, length us, event | category | flops | bytes accessed | tf_op | source)
XLA Modules:
  0.0 199.0 jit_solution(11254666562262782839)
XLA Ops:
  0.6 1.2 convert_bitcast_fusion.pos
  1.8 49.0 %shard_map.195 = (bf16[128,256]{1,0:T(8,128)(2,1)}, f32[8,128]{1,0:T(8,128)}, bf16[8,128,128]{2,1,0:T(8,128)(2,1)}, bf16[8,128,128]{2,1,0:T(8,128)(2,1)}, bf16[8...) custom-call(bf16[128,1024]{1,0:T(8,128)(2,1)} %keys.1, ...), custom_call_target="tpu_custom_call" | custom-call | tf_op jit(solution)/shard_map/pallas_call | solution.py:425
  50.8 3.6 %fusion.7 = f32[128,448]{0,1:T(8,128)S(1)} fusion(bf16[4096,448]{0,1:T(8,128)(2,1)} %param.19, bf16[16,8,4096]{2,1,0:T(8,128)(2,1)} %get-tuple-element.33.nrm_all), kind=kOutput, calls=%fused_computation.9 | convolution fusion | flops 469762048 | bytes 4947968 | tf_op jit(solution)/shard_map/dot_general | solution.py:473
  54.4 0.1 copy.36
  54.6 3.2 %fusion.11 = (f32[128,448]{0,1:T(8,128)S(1)}, f32[128,448]{0,1:T(8,128)S(1)}) fusion(f32[128,448]{0,1:T(8,128)S(1)} %fusion.7, bf16[448,4096]{1,0:T(8,128)(2,1)} %param.20, bf16[16,8,4096]{2,1,0:T(8,128)(2,1)S(1)} %copy-done.3), kind=kOutput, calls=%fused_computation.19 | convolution fusion | flops 469819392 | bytes 5406720 | tf_op jit(solution)/shard_map/dot_general | solution.py:477
  57.8 0.1 copy.31
  58.0 0.1 copy.33
  58.1 3.5 %multiply_convert_fusion = (bf16[128,448]{1,0:T(8,128)(2,1)S(1)}, bf16[128,448]{1,0:T(8,128)(2,1)S(1)}, bf16[128,448]{1,0:T(8,128)(2,1)S(1)}) fusion(f32[128,448]{1,0:T(8,128)S(1)} %copy.36, f32[128,448]{1,0:T(8,128)S(1)} %copy.31, f32[128,448]{1,0:T(8,128)S(1)} %copy.33, bf16[4096,448]{0,1:T(8,128)(2,1)} %param.18, bf16[16,8,4096]{2,1,0:T(8,128)(2,1)S(1)} %copy-done.2), kind=kOutput, calls=%fused_computation.13 | convolution fusion | flops 470622208 | bytes 5750784 | tf_op jit(solution)/shard_map/dot_general | solution.py:472
  61.7 0.8 pad_maximum_fusion.gu
  62.5 1.8 convolution_convert_fusion
  64.2 0.7 fusion.12
  65.0 1.3 copy-done.1
  66.3 1.7 fusion
  68.0 117.5 %shard_map.196 = (bf16[8,4096]{1,0:T(8,128)(2,1)}, bf16[8,4096]{1,0:T(8,128)(2,1)}, bf16[128,256]{1,0:T(8,128)(2,1)}, f32[8,1024]{1,0:T(8,128)}, f32[8,1024]{1,0...) custom-call(bf16[8,2,8,4096]{3,2,1,0:T(8,128)(2,1)} %bitcast.41, ...), custom_call_target="tpu_custom_call" | custom-call | tf_op jit(solution)/shard_map/pallas_call | solution.py:425
  185.4 2.8 %fusion.13 = f32[256,512]{1,0:T(8,128)} fusion(bf16[1024,256]{1,0:T(8,128)(2,1)} %bitcast.43, bf16[1024,512]{1,0:T(8,128)(2,1)} %bitcast.42), kind=kOutput, calls=%fused_computation.21 | convolution fusion | flops 268435456 | bytes 2097152 | tf_op jit(solution)/shard_map/dot_general | solution.py:534
  188.2 3.8 %fusion.1 = f32[512,448]{0,1:T(8,128)} fusion(bf16[1024,512]{1,0:T(8,128)(2,1)} %bitcast.53, bf16[1024,896]{1,0:T(8,128)(2,1)} %bitcast.49), kind=kOutput, calls=%fused_computation.3 | convolution fusion | flops 469762048 | bytes 3014656 | tf_op jit(solution)/shard_map/dot_general | solution.py:536
  192.1 1.6 fusion.3
  193.7 1.6 fusion.14
  195.3 0.6 copy.44
  195.9 0.6 copy.45
  196.6 0.6 copy.46
  197.2 0.6 copy.47
  197.8 0.6 copy.48
  198.4 0.6 copy.49
  (31 shorter events, 0.1 us)
Async XLA Ops:
  50.8 3.7 %copy-start.3 = (bf16[16,8,4096]{2,1,0:T(8,128)(2,1)S(1)}, bf16[16,8,4096]{2,1,0:T(8,128)(2,1)}, u32[]{:S(2)}) copy-start(bf16[16,8,4096]{2,1,0:T(8,128)(2,1)} %get-tuple-element.32.cot_all) | copy-start | bytes 3145732
  54.4 3.7 %copy-start.2 = (bf16[16,8,4096]{2,1,0:T(8,128)(2,1)S(1)}, bf16[16,8,4096]{2,1,0:T(8,128)(2,1)}, u32[]{:S(2)}) copy-start(bf16[16,8,4096]{2,1,0:T(8,128)(2,1)} %get-tuple-element.33.nrm_all) | copy-start | bytes 3145732
  58.1 4.4 %copy-start = (bf16[448,4096]{1,0:T(8,128)(2,1)S(1)}, bf16[448,4096]{1,0:T(8,128)(2,1)}, u32[]{:S(2)}) copy-start(bf16[448,4096]{1,0:T(8,128)(2,1)} %param.20) | copy-start | bytes 11010052
  61.6 3.3 %copy-start.5 = (bf16[128,448]{1,0:T(8,128)(2,1)}, bf16[128,448]{1,0:T(8,128)(2,1)S(1)}, u32[]{:S(2)}) copy-start(bf16[128,448]{1,0:T(8,128)(2,1)S(1)} %get-tuple-element.54.act) | copy-start | bytes 344068
  61.7 2.6 %copy-start.4 = (bf16[4096,448]{0,1:T(8,128)(2,1)S(1)}, bf16[4096,448]{0,1:T(8,128)(2,1)}, u32[]{:S(2)}) copy-start(bf16[4096,448]{0,1:T(8,128)(2,1)} %param.18) | copy-start | bytes 11010052
  64.2 2.0 %copy-start.1 = (bf16[4096,448]{0,1:T(8,128)(2,1)S(1)}, bf16[4096,448]{0,1:T(8,128)(2,1)}, u32[]{:S(2)}) copy-start(bf16[4096,448]{0,1:T(8,128)(2,1)} %param.19) | copy-start | bytes 11010052
  185.4 6.6 %copy-start.12 = (bf16[8,128,896]{2,1,0:T(8,128)(2,1)S(1)}, bf16[8,128,896]{2,1,0:T(8,128)(2,1)}, u32[]{:S(2)}) copy-start(bf16[8,128,896]{2,1,0:T(8,128)(2,1)} %get-tuple-element.51) | copy-start | bytes 5505028
  185.4 6.6 %copy-start.15 = (bf16[8,16,8,512]{3,2,1,0:T(8,128)(2,1)S(1)}, bf16[8,16,8,512]{3,2,1,0:T(8,128)(2,1)}, u32[]{:S(2)}) copy-start(bf16[8,16,8,512]{3,2,1,0:T(8,128)(2,1)} %get-tuple-element.50) | copy-start | bytes 3145732
  188.2 5.5 %copy-start.13 = (bf16[8,16,8,512]{3,2,1,0:T(8,128)(2,1)S(1)}, bf16[8,16,8,512]{3,2,1,0:T(8,128)(2,1)}, u32[]{:S(2)}) copy-start(bf16[8,16,8,512]{3,2,1,0:T(8,128)(2,1)} %get-tuple-element.53) | copy-start | bytes 3145732
  188.2 5.5 %copy-start.14 = (bf16[8,128,448]{2,1,0:T(8,128)(2,1)S(1)}, bf16[8,128,448]{2,1,0:T(8,128)(2,1)}, u32[]{:S(2)}) copy-start(bf16[8,128,448]{2,1,0:T(8,128)(2,1)} %get-tuple-element.52) | copy-start | bytes 2752516
  192.0 3.3 %copy-start.8 = (bf16[8,4096]{1,0:T(8,128)(2,1)S(1)}, bf16[8,4096]{1,0:T(8,128)(2,1)}, u32[]{:S(2)}) copy-start(bf16[8,4096]{1,0:T(8,128)(2,1)} %get-tuple-element.69) | copy-start | bytes 196612
  192.0 3.9 %copy-start.7 = (bf16[8,4096]{1,0:T(8,128)(2,1)S(1)}, bf16[8,4096]{1,0:T(8,128)(2,1)}, u32[]{:S(2)}) copy-start(bf16[8,4096]{1,0:T(8,128)(2,1)} %get-tuple-element.70) | copy-start | bytes 196612
  192.0 4.5 %copy-start.6 = (bf16[128,256]{1,0:T(8,128)(2,1)S(1)}, bf16[128,256]{1,0:T(8,128)(2,1)}, u32[]{:S(2)}) copy-start(bf16[128,256]{1,0:T(8,128)(2,1)} %get-tuple-element.71) | copy-start | bytes 196612
  192.1 5.1 %copy-start.10 = (f32[8,1024]{1,0:T(8,128)S(1)}, f32[8,1024]{1,0:T(8,128)}, u32[]{:S(2)}) copy-start(f32[8,1024]{1,0:T(8,128)} %get-tuple-element.72) | copy-start | bytes 98308
  192.1 5.7 %copy-start.9 = (f32[8,1024]{1,0:T(8,128)S(1)}, f32[8,1024]{1,0:T(8,128)}, u32[]{:S(2)}) copy-start(f32[8,1024]{1,0:T(8,128)} %get-tuple-element.73) | copy-start | bytes 98308
  193.7 4.7 %copy-start.11 = (f32[1,4096]{1,0:T(1,128)S(1)}, f32[1,4096]{1,0:T(1,128)}, u32[]{:S(2)}) copy-start(f32[1,4096]{1,0:T(1,128)} %get-tuple-element.47) | copy-start | bytes 49156

commit v2 on v1

v2 whole, which is shorter than its diff:
```python
import functools
import math

import jax
import jax.numpy as jnp
from jax import lax
from jax.experimental import pallas as pl
from jax.experimental.pallas import tpu as pltpu
from jax.sharding import PartitionSpec as P

MESH = pl.DeviceIdType.MESH
F32 = jnp.float32
BF = jnp.bfloat16
CTX = 8
CHIPS = 8
HW = 128
SCALE = 1.0 / math.sqrt(128)
NEG = -1e30
EPS = 1e-05
NT = (((1,), (1,)), ((), ()))


CHUNKS = 2
WIDE = 4096 // CHUNKS
FAR = [(1, 0), (3, 0), (0, 1), (1, 1), (3, 1), (2, 0), (2, 1)]


class Net:
    def __init__(self, ssem, rsem):
        self.ssem, self.rsem, self.used = ssem, rsem, 0
        self.sent = []
        self.c = lax.axis_index("ctx")
        self.f = lax.axis_index("ffn")
        self.core = lax.rem(self.f, 2)
        self.chip = self.f // 2
        self.partner = self.f + 1 - 2 * self.core

    def copy(self, src, dst, c=None, f=None):
        n = self.used
        self.used = n + 1
        cp = pltpu.make_async_remote_copy(
            src_ref=src,
            dst_ref=dst,
            send_sem=self.ssem.at[n],
            recv_sem=self.rsem.at[n],
            device_id=(self.c if c is None else c, self.f if f is None else f),
            device_id_type=MESH,
        )
        self.sent.append(cp)
        return cp

    def local(self, src, dst):
        n = self.used
        self.used = n + 1
        return pltpu.make_async_copy(src, dst, self.rsem.at[n])

    def done(self, copies):
        for cp in copies:
            cp.wait_send()
            self.sent = [s for s in self.sent if s is not cp]

    def drain(self):
        self.done(list(self.sent))

    def ctx_at(self, d):
        x, y = self.c // 2, lax.rem(self.c, 2)
        return lax.rem(x + d[0], 4) * 2 + lax.rem(y + d[1], 2)

    def ctx_from(self, d):
        return self.ctx_at((4 - d[0], d[1]))

    def chip_at(self, d):
        z, y = self.chip // 2, lax.rem(self.chip, 2)
        return lax.rem(z + d[0], 4) * 2 + lax.rem(y + d[1], 2)

    def chip_from(self, d):
        return self.chip_at((4 - d[0], d[1]))

    def greet(self):
        barrier = pltpu.get_barrier_semaphore()
        for d in FAR:
            pl.semaphore_signal(
                barrier, inc=1, device_id=(self.ctx_at(d), self.f), device_id_type=MESH
            )
        for k in range(1, 16):
            pl.semaphore_signal(
                barrier,
                inc=1,
                device_id=(self.c, lax.rem(self.f + k, 16)),
                device_id_type=MESH,
            )
        pl.semaphore_wait(barrier, 22)


def start_all(copies):
    for cp in copies:
        cp.start()


def wait_all(copies):
    for cp in copies:
        cp.wait_recv()


def ctx_gather(net, src, dst):
    return [net.copy(src, dst.at[net.c], c=net.ctx_at(d)) for d in FAR]


class CtxRelay:
    def __init__(self, net, src, buf):
        self.net, self.buf = net, buf
        mine = buf.at[net.c]
        self.pair = net.copy(src, mine, c=net.ctx_at((0, 1)))
        self.up = net.copy(src, mine, c=net.ctx_at((1, 0)))
        self.down = net.copy(src, mine, c=net.ctx_at((3, 0)))

    def start(self):
        self.pair.start()
        self.up.start()
        self.down.start()

    def pump(self):
        net, buf = self.net, self.buf
        self.pair.wait_recv()
        other = buf.at[net.ctx_at((0, 1))]
        self.up2 = net.copy(other, other, c=net.ctx_at((1, 0)))
        self.down2 = net.copy(other, other, c=net.ctx_at((3, 0)))
        self.up2.start()
        self.down2.start()
        self.up.wait_recv()
        below = buf.at[net.ctx_at((3, 0))]
        self.up3 = net.copy(below, below, c=net.ctx_at((1, 0)))
        self.up3.start()
        self.down2.wait_recv()
        above = buf.at[net.ctx_at((1, 1))]
        self.down3 = net.copy(above, above, c=net.ctx_at((3, 0)))
        self.down3.start()

    def finish(self):
        wait_all([self.down, self.up2, self.up3, self.down3])


class CtxColumns:
    def __init__(self, net, src, dst):
        self.net, self.dst = net, dst
        half = pl.ds(net.core * 8, 8)
        self.half = half
        self.far = []
        for d in FAR:
            to = net.ctx_at(d)
            cols = pl.ds(pl.multiple_of(to * 512, 512), 512)
            self.far.append(net.copy(src.at[half, :, cols], dst.at[net.c, half], c=to))

    def start(self):
        start_all(self.far)

    def forward(self):
        net = self.net
        self.near = []
        for d, cp in zip(FAR, self.far):
            cp.wait_recv()
            block = self.dst.at[net.ctx_from(d), self.half]
            near = net.copy(block, block, f=net.partner)
            near.start()
            self.near.append(near)

    def finish(self):
        wait_all(self.near)


class FfnGather:
    def __init__(self, net, src, dst):
        self.net, self.dst = net, dst
        self.far = [net.copy(src, dst.at[net.f], f=net.chip_at(d) * 2 + net.core) for d in FAR]
        self.near = [net.copy(src, dst.at[net.f], f=net.partner)]

    def start(self):
        start_all(self.far)
        self.near[0].start()

    def forward(self):
        net = self.net
        for d, cp in zip(FAR, self.far):
            cp.wait_recv()
            block = self.dst.at[net.chip_from(d) * 2 + net.core]
            near = net.copy(block, block, f=net.partner)
            near.start()
            self.near.append(near)

    def finish(self):
        wait_all(self.near)


class FfnScatter:
    def __init__(self, net, part, pair_in, summed, got):
        self.net, self.part, self.pair_in, self.summed, self.got = net, part, pair_in, summed, got
        self.pair, self.far = [], []
        for n in range(CHUNKS):
            span = pl.ds(n * WIDE, WIDE)
            self.pair.append(
                net.copy(
                    part.at[:, 1 - net.core, :, span], pair_in.at[:, :, span], f=net.partner
                )
            )
            self.far.append(
                [
                    net.copy(
                        summed.at[net.chip_at(d), :, span],
                        got.at[net.chip, :, span],
                        f=net.chip_at(d) * 2 + net.core,
                    )
                    for d in FAR
                ]
            )

    def put(self, n, product):
        for b in range(16):
            self.part[b // 2, b % 2, :, n * WIDE : (n + 1) * WIDE] = product[
                b * 8 : (b + 1) * 8
            ].astype(BF)
        self.pair[n].start()

    def chip_sum(self, to, n):
        span = slice(n * WIDE, (n + 1) * WIDE)
        return self.part[to, self.net.core, :, span].astype(F32) + self.pair_in[
            to, :, span
        ].astype(F32)

    def middle(self, n):
        net = self.net
        self.pair[n].wait_recv()
        for d, cp in zip(FAR, self.far[n]):
            to = net.chip_at(d)
            self.summed[to, :, n * WIDE : (n + 1) * WIDE] = self.chip_sum(to, n).astype(BF)
            cp.start()

    def finish(self):
        net = self.net
        pieces = []
        for n in range(CHUNKS):
            total = self.chip_sum(net.chip, n)
            for d, cp in zip(FAR, self.far[n]):
                cp.wait_recv()
                total = total + self.got[
                    net.chip_from(d), :, n * WIDE : (n + 1) * WIDE
                ].astype(F32)
            pieces.append(total)
        return jnp.concatenate(pieces, axis=1)

    def drain(self):
        self.net.done(self.pair + [cp for far in self.far for cp in far])


def seg_starts(doc_ref, pos):
    doc = doc_ref[...]
    start = jnp.zeros_like(pos)
    for v in (1, 2, 3):
        edge = jnp.sum((doc < v).astype(F32))
        start = jnp.where(pos >= edge, jnp.maximum(start, edge), start)
    return start


def as_column(row):
    return jnp.transpose(jnp.broadcast_to(row, (128, 128)))


def as_row(column):
    return jnp.transpose(jnp.broadcast_to(column, (128, 128)))[0:1, :]


def layer(
    keys, values, q, pos, doc, resid, gain, cot, wout_h, wgate_h, wup_h, wdown_h,
    mixed, gres, dq, kg, vg, gg, nrm_c, cot_c, gres_c, gate_all, up_all, act_all, att_all,
    wout, wgate, wup, wdown, att, kv_all, q_all, pos_all, nrm_all, cot_all, grows, xr, gact,
    part, pair_in, summed, got, part2, pair_in2, summed2, got2,
    nbuf, gbuf, act, ggate, gup, ga, ga_all, stats, stats_all,
    kv, kv_in, gsum, gpair, gchip, gctx_b, gctx, ssem, rsem,
):
    net = Net(ssem, rsem)
    c, f = net.c, net.f
    cols = pl.ds(pl.multiple_of(net.chip * 128, 128), 128)
    kv_all[0, c] = keys[:, cols]
    kv_all[1, c] = values[:, cols]
    pos_all[c] = pos[...]
    loads = [
        net.local(wout_h, wout),
        net.local(wdown_h, wdown),
        net.local(wgate_h, wgate),
        net.local(wup_h, wup),
    ]
    start_all(loads)
    net.greet()
    mine = kv_all.at[net.core, c]
    kv_far = [net.copy(mine, mine, c=net.ctx_at(d)) for d in FAR]
    pos_far = ctx_gather(net, pos, pos_all)
    start_all(kv_far)
    start_all(pos_far)
    q_all[c] = q[...]
    cot_all[f] = cot[...]
    cot_ag = FfnGather(net, cot, cot_all)
    q_ag = CtxRelay(net, q, q_all)
    kv_near = []
    for d, cp in zip(FAR, kv_far):
        cp.wait_recv()
        block = kv_all.at[net.core, net.ctx_from(d)]
        near = net.copy(block, block, f=net.partner)
        near.start()
        kv_near.append(near)
    cot_ag.start()
    wait_all(pos_far)
    wait_all(kv_near)
    q_ag.start()
    kpos = jnp.concatenate([pos_all[i] for i in range(CTX)], axis=1)
    qpos = as_column(pos[...])[:, 0:1]
    visible = (kpos <= qpos) & (kpos >= seg_starts(doc, qpos))
    k = kv_all[0].reshape(1024, 128)
    v = kv_all[1].reshape(1024, 128)
    lcol = []
    for h in range(2):
        hs = slice(h * 128, (h + 1) * 128)
        s = lax.dot_general(q[:, hs], k, NT, preferred_element_type=F32) * SCALE
        s = jnp.where(visible, s, NEG)
        top = jnp.max(s, axis=1, keepdims=True)
        w = jnp.where(visible, jnp.exp(s - top), 0.0)
        total = jnp.sum(w, axis=1, keepdims=True)
        o = jnp.dot(w.astype(BF), v, preferred_element_type=F32) / total
        att[:, hs] = o.astype(BF)
        lcol.append(top + jnp.log(total))
    a = att[...]
    loads[0].wait()
    rs = FfnScatter(net, part, pair_in, summed, got)
    for n in range(CHUNKS):
        rs.put(n, jnp.dot(a, wout[:, n * WIDE : (n + 1) * WIDE], preferred_element_type=F32))
    att_all[c] = a
    att_ag = CtxRelay(net, att, att_all)
    for n in range(CHUNKS):
        rs.middle(n)
    cot_ag.forward()
    q_ag.pump()
    att_ag.start()
    cot_ag.finish()
    loads[1].wait()
    rows = jnp.concatenate([cot_all[b] for b in range(16)], axis=0)
    gact[...] = lax.dot_general(rows, wdown[...], NT, preferred_element_type=F32)
    own = pl.ds(pl.multiple_of(c * 512, 512), 512)
    cot_c[c] = cot_all[:, :, own]
    cot_cols = CtxColumns(net, cot_all, cot_c)
    projected = rs.finish()
    hidden = (resid[...].astype(F32) + projected).astype(BF)
    hf = hidden.astype(F32)
    ir = lax.rsqrt(jnp.mean(hf * hf, axis=1, keepdims=True) + EPS)
    normed = (hf * ir * gain[...]).astype(BF)
    nbuf[...] = normed
    nrm_all[f] = normed
    ag = FfnGather(net, nbuf, nrm_all)
    ag.start()
    cot_cols.start()
    ag.forward()
    att_ag.pump()
    ag.finish()
    nrm_cols = CtxColumns(net, nrm_all, nrm_c)
    nrm_cols.start()
    nrm_c[c] = nrm_all[:, :, own]
    xr[...] = jnp.concatenate([nrm_all[b] for b in range(16)], axis=0)
    loads[2].wait()
    gate_pre = jnp.dot(xr[...], wgate[...], preferred_element_type=F32)
    loads[3].wait()
    up_proj = jnp.dot(xr[...], wup[...], preferred_element_type=F32)
    sig = jax.nn.sigmoid(gate_pre)
    grad_act = gact[...]
    activated = (gate_pre * sig * up_proj).astype(BF)
    grad_up = (grad_act * gate_pre * sig).astype(BF)
    grad_gate = (grad_act * up_proj * sig * (1.0 + gate_pre * (1.0 - sig))).astype(BF)
    act[...] = activated
    ggate[...] = grad_gate
    gup[...] = grad_up
    rs.drain()
    rs = FfnScatter(net, part, pair_in, summed, got)
    for n in range(CHUNKS):
        span = slice(n * WIDE, (n + 1) * WIDE)
        rs.put(
            n,
            lax.dot_general(ggate[...], wgate[span, :], NT, preferred_element_type=F32)
            + lax.dot_general(gup[...], wup[span, :], NT, preferred_element_type=F32),
        )
    gate_all[c] = ggate[...]
    up_all[c] = gup[...]
    act_all[c] = act[...]
    gate_ag = CtxRelay(net, ggate, gate_all)
    up_ag = CtxRelay(net, gup, up_all)
    act_ag = CtxRelay(net, act, act_all)
    gate_ag.start()
    up_ag.start()
    act_ag.start()
    for n in range(CHUNKS):
        rs.middle(n)
    cot_cols.forward()
    nrm_cols.forward()
    rs2 = FfnScatter(net, part2, pair_in2, summed2, got2)
    for n in range(CHUNKS):
        rs2.put(
            n, jnp.dot(act[...], wdown[:, n * WIDE : (n + 1) * WIDE], preferred_element_type=F32)
        )
    gate_ag.pump()
    gnorm = rs.finish()
    gained = gnorm * gain[...]
    cube = ir * ir * ir
    mean = jnp.mean(gained * hf, axis=1, keepdims=True)
    gr = (cot[...].astype(F32) + ir * gained - hf * cube * mean).astype(BF)
    gres[...] = gr
    gbuf[...] = gr
    grows[f] = gr
    gsum[...] = jnp.sum(gnorm * hf * ir, axis=0, keepdims=True)
    ag = FfnGather(net, gbuf, grows)
    ag.start()
    g1 = net.copy(gsum, gpair, f=net.partner)
    g1.start()
    up_ag.pump()
    g1.wait_recv()
    gchip[net.chip] = gsum[...] + gpair[...]
    g2 = [
        net.copy(gchip.at[net.chip], gchip.at[net.chip], f=net.chip_at(d) * 2 + net.core)
        for d in FAR
    ]
    start_all(g2)
    ag.forward()
    ag.finish()
    for n in range(CHUNKS):
        rs2.middle(n)
    rows = jnp.concatenate([grows[b] for b in range(16)], axis=0)
    gat = lax.dot_general(rows, wout[...], NT, preferred_element_type=F32).astype(BF)
    ga[...] = gat
    ga_all[c] = gat
    prod = gat.astype(F32) * att[...].astype(F32)
    delta = [jnp.sum(prod[:, h * 128 : (h + 1) * 128], axis=1, keepdims=True) for h in range(2)]
    st = jnp.concatenate(
        [as_row(r) for r in lcol + delta] + [jnp.zeros((4, 128), F32)], axis=0
    )
    stats[...] = st
    stats_all[c] = st
    late = ctx_gather(net, ga, ga_all) + ctx_gather(net, stats, stats_all)
    start_all(late)
    gres_cols = CtxColumns(net, grows, gres_c)
    gres_cols.start()
    gres_c[c] = grows[:, :, own]
    act_ag.pump()
    k = kv_all[0].reshape(1024, 128)
    v = kv_all[1].reshape(1024, 128)
    for h in range(2):
        hs = slice(h * 128, (h + 1) * 128)
        s = lax.dot_general(q[:, hs], k, NT, preferred_element_type=F32) * SCALE
        p = jnp.where(visible, jnp.exp(jnp.where(visible, s, NEG) - lcol[h]), 0.0)
        dp = lax.dot_general(ga[:, hs], v, NT, preferred_element_type=F32)
        ds = (p * (dp - delta[h])).astype(BF)
        dq[:, hs] = (jnp.dot(ds, k, preferred_element_type=F32) * SCALE).astype(BF)
    wait_all(g2)
    tot = gchip[0]
    for i in range(1, CHIPS):
        tot = tot + gchip[i]
    gctx_b[...] = tot
    gctx[c] = tot
    g3 = ctx_gather(net, gctx_b, gctx)
    start_all(g3)
    q_ag.finish()
    wait_all(late)
    vis_t = (qpos <= kpos) & (qpos >= seg_starts(doc, kpos))
    k_own = kv_all[0, c]
    v_own = kv_all[1, c]
    dk = jnp.zeros((128, 128), F32)
    dv = jnp.zeros((128, 128), F32)
    for h in range(2):
        hs = slice(h * 128, (h + 1) * 128)
        qa = q_all[:, :, hs].reshape(1024, 128)
        gaa = ga_all[:, :, hs].reshape(1024, 128)
        lrow = jnp.concatenate([stats_all[i, h : h + 1, :] for i in range(CTX)], axis=1)
        drow = jnp.concatenate([stats_all[i, 2 + h : 3 + h, :] for i in range(CTX)], axis=1)
        s = lax.dot_general(k_own, qa, NT, preferred_element_type=F32) * SCALE
        p = jnp.where(vis_t, jnp.exp(jnp.where(vis_t, s, NEG) - lrow), 0.0)
        dp = lax.dot_general(v_own, gaa, NT, preferred_element_type=F32)
        ds = (p * (dp - drow)).astype(BF)
        dk = dk + jnp.dot(ds, qa, preferred_element_type=F32)
        dv = dv + jnp.dot(p.astype(BF), gaa, preferred_element_type=F32)
    dkv = jnp.concatenate([dk * SCALE, dv], axis=1)
    for b in range(16):
        kv[b] = dkv[b * 8 : (b + 1) * 8]
    kv_in[f] = kv[f]
    last = []
    for n in range(1, 16):
        to = lax.rem(f + n, 16)
        last.append(net.copy(kv.at[to], kv_in.at[f], f=to))
    start_all(last)
    gres_cols.forward()
    mixed[...] = (hf + rs2.finish()).astype(BF)
    wait_all(g3)
    tot = gctx[0]
    for i in range(1, CTX):
        tot = tot + gctx[i]
    gg[...] = tot
    wait_all(last)
    for g in range(8):
        pair = kv_in[2 * g] + kv_in[2 * g + 1]
        kg[:, g * 128 : (g + 1) * 128] = pair[:, 0:128]
        vg[:, g * 128 : (g + 1) * 128] = pair[:, 128:256]
    for gather in (cot_cols, nrm_cols, gres_cols, gate_ag, up_ag, act_ag, att_ag):
        gather.finish()
    net.drain()


VM = pl.BlockSpec(memory_space=pltpu.VMEM)
ANY = pl.BlockSpec(memory_space=pl.ANY)
SEMS = 320


def body(
    resid_in, queries, keys_in, value_rows_input, w_out, norm_gain, w_gate, w_up, w_down,
    cotangent, positions, doc_ids,
):
    pos = positions.astype(F32).reshape(1, 128)
    doc = doc_ids.reshape(8, 128)
    gain = norm_gain.reshape(1, 4096)
    outs = [
        ((8, 4096), BF),
        ((8, 4096), BF),
        ((128, 256), BF),
        ((8, 1024), F32),
        ((8, 1024), F32),
        ((1, 4096), F32),
        ((8, 16, 8, 512), BF),
        ((8, 16, 8, 512), BF),
        ((8, 16, 8, 512), BF),
        ((8, 128, 448), BF),
        ((8, 128, 448), BF),
        ((8, 128, 448), BF),
        ((8, 128, 256), BF),
    ]
    scratch = [
        ((256, 4096), BF),
        ((4096, 448), BF),
        ((4096, 448), BF),
        ((448, 4096), BF),
        ((128, 256), BF),
        ((2, 8, 128, 128), BF),
        ((8, 128, 256), BF),
        ((8, 1, 128), F32),
        ((16, 8, 4096), BF),
        ((16, 8, 4096), BF),
        ((16, 8, 4096), BF),
        ((128, 4096), BF),
        ((128, 448), F32),
    ]
    scratch += [((8, 2, 8, 4096), BF)] + [((8, 8, 4096), BF)] * 3
    scratch += [((8, 2, 8, 4096), BF)] + [((8, 8, 4096), BF)] * 3
    scratch += [
        ((8, 4096), BF),
        ((8, 4096), BF),
        ((128, 448), BF),
        ((128, 448), BF),
        ((128, 448), BF),
        ((128, 256), BF),
        ((8, 128, 256), BF),
        ((8, 128), F32),
        ((8, 8, 128), F32),
        ((16, 8, 256), F32),
        ((16, 8, 256), F32),
        ((1, 4096), F32),
        ((1, 4096), F32),
        ((8, 1, 4096), F32),
        ((1, 4096), F32),
        ((8, 1, 4096), F32),
    ]
    (mixed, gres, dq, kg, vg, gg, nrm_c, cot_c, gres_c, gate_all, up_all, act_all, att_all) = (
        pl.pallas_call(
            layer,
            out_shape=[jax.ShapeDtypeStruct(s, d) for s, d in outs],
            in_specs=[VM] * 8 + [ANY] * 4,
            out_specs=[VM] * len(outs),
            scratch_shapes=[pltpu.VMEM(s, d) for s, d in scratch]
            + [pltpu.SemaphoreType.DMA((SEMS,)), pltpu.SemaphoreType.DMA((SEMS,))],
            compiler_params=pltpu.CompilerParams(
                collective_id=0, has_side_effects=True, vmem_limit_bytes=60 * 2**20
            ),
        )(
            keys_in, value_rows_input, queries, pos, doc, resid_in, gain, cotangent,
            w_out, w_gate, w_up, w_down,
        )
    )
    contract = functools.partial(
        lax.dot_general,
        dimension_numbers=(((0,), (0,)), ((), ())),
        preferred_element_type=F32,
    )
    nrm_c = nrm_c.reshape(1024, 512)
    grad_w_out = contract(att_all.reshape(1024, 256), gres_c.reshape(1024, 512))
    grad_w_gate = contract(nrm_c, gate_all.reshape(1024, 448))
    grad_w_up = contract(nrm_c, up_all.reshape(1024, 448))
    grad_w_down = contract(act_all.reshape(1024, 448), cot_c.reshape(1024, 512))
    return (
        mixed, gres, dq, kg, vg, gg.reshape(4096), grad_w_out, grad_w_gate, grad_w_up, grad_w_down,
    )


def solution(mesh):
    rows = P(("ctx", "ffn"), None)
    return jax.shard_map(
        body,
        mesh=mesh,
        in_specs=(
            rows, P("ctx", "ffn"), P("ctx", None), P("ctx", None), P("ffn", None), P(),
            P(None, "ffn"), P(None, "ffn"), P("ffn", None), rows, P("ctx"), P(),
        ),
        out_specs=(
            rows, rows, P("ctx", "ffn"), rows, rows, P(), P("ffn", "ctx"), P("ctx", "ffn"),
            P("ctx", "ffn"), P("ffn", "ctx"),
        ),
        check_vma=False,
    )
```

time: 199 us -> 142 us (0.71)
  Pallas kernels: 166 us -> 114 us
  matrix products: 24.3 us -> 9.14 us
  local copies, waits for them, and re-layouts: 5.45 us -> 16.6 us
    pallas_call x2 -> x1, Pallas kernels: 166 us -> 114 us  [body(): pl.pallas_call(layer, out_shape=[jax.ShapeDtypeStruct(s, d) for s, d in o...]
    dot_general x10 -> x4, matrix products: 24.3 us -> 9.14 us  [the longest x1 3.15 us: body(): grad_w_up = contract(nrm_c, up_all.reshape(1024, 448))]
    unnamed x38 -> x28, local copies, waits for them, and re-layouts: 5.06 us -> 16.6 us
where the time goes in v2:
time: 142 us
  Pallas kernels  114 us (80%)
  local copies, waits for them, and re-layouts  16.6 us (12%)
  matrix products  9.14 us (6%)
    pallas_call x1, Pallas kernels, body(): pl.pallas_call(layer, out_shape=[jax.ShapeDtypeStruct(s, d) for s, d in o...  114 us
    unnamed x28, local copies, waits for them, and re-layouts  16.6 us
    dot_general x1, matrix products, body(): grad_w_up = contract(nrm_c, up_all.reshape(1024, 448))  3.15 us

profile of v2, /device:TPU:1, one launch (start us, length us, event | category | flops | bytes accessed | tf_op | source)
XLA Modules:
  0.0 142.1 jit_solution(8568608046734854162)
XLA Ops:
  0.6 1.2 convert_bitcast_fusion.pos
  1.8 6.4 %copy.22.wgate_h = bf16[4096,448]{1,0:T(8,128)(2,1)} copy(bf16[4096,448]{0,1:T(8,128)(2,1)} %param.18) | data formatting | bytes 7340032 | tf_op args[6]
  8.2 6.4 %copy.23.wup_h = bf16[4096,448]{1,0:T(8,128)(2,1)} copy(bf16[4096,448]{0,1:T(8,128)(2,1)} %param.19) | data formatting | bytes 7340032 | tf_op args[7]
  14.7 114.4 %shard_map.195 = (bf16[8,4096]{1,0:T(8,128)(2,1)}, bf16[8,4096]{1,0:T(8,128)(2,1)}, bf16[128,256]{1,0:T(8,128)(2,1)}, f32[8,1024]{1,0:T(8,128)}, f32[8,1024]{1,0...) custom-call(bf16[128,1024]{1,0:T(8,128)(2,1)} %keys.1, ...), custom_call_target="tpu_custom_call" | custom-call | tf_op jit(solution)/shard_map/pallas_call | solution.py:572
  129.1 0.0 copy-start.8
  129.1 0.0 copy-start.9
  129.1 0.0 copy-start.6
  129.1 0.0 copy-start.7
  129.1 2.8 %fusion = f32[256,512]{1,0:T(8,128)} fusion(bf16[1024,256]{1,0:T(8,128)(2,1)} %bitcast.21, bf16[1024,512]{1,0:T(8,128)(2,1)} %bitcast.20), kind=kOutput, calls=%fused_computation.1 | convolution fusion | flops 268435456 | bytes 2097152 | tf_op jit(solution)/shard_map/dot_general | solution.py:593
  131.9 3.2 %fusion.2 = f32[512,448]{0,1:T(8,128)} fusion(bf16[1024,512]{1,0:T(8,128)(2,1)} %bitcast.27, bf16[1024,448]{1,0:T(8,128)(2,1)} %bitcast.30), kind=kOutput, calls=%fused_computation.3 | convolution fusion | flops 469762048 | bytes 2883584 | tf_op jit(solution)/shard_map/dot_general | solution.py:595
  135.1 0.0 copy-done.8
  135.1 0.0 copy-done.9
  135.1 0.0 copy-start.1
  135.1 0.0 copy-start
  135.1 1.6 %fusion.1 = f32[512,448]{0,1:T(8,128)} fusion(bf16[1024,512]{1,0:T(8,128)(2,1)S(1)} %bitcast.28, bf16[1024,448]{1,0:T(8,128)(2,1)S(1)} %bitcast.29), kind=kOutput, calls=%fused_computation.2 | convolution fusion | flops 469762048 | bytes 2883584 | tf_op jit(solution)/shard_map/dot_general | solution.py:594
  136.7 1.6 %fusion.3 = f32[448,512]{1,0:T(8,128)} fusion(bf16[1024,448]{1,0:T(8,128)(2,1)S(1)} %bitcast.26, bf16[1024,512]{1,0:T(8,128)(2,1)S(1)} %bitcast.25), kind=kOutput, calls=%fused_computation.4 | convolution fusion | flops 469762048 | bytes 2883584 | tf_op jit(solution)/shard_map/dot_general | solution.py:596
  138.3 0.6 copy.30
  139.0 0.0 copy-done.1
  139.0 0.6 copy.31
  139.6 0.6 copy.32
  140.2 0.0 copy-done.4
  140.2 0.6 copy.33
  140.8 0.6 copy.34
  141.5 0.6 copy.35
  (10 shorter events, 0.0 us)
Async XLA Ops:
  129.1 6.0 %copy-start.8 = (bf16[8,16,8,512]{3,2,1,0:T(8,128)(2,1)S(1)}, bf16[8,16,8,512]{3,2,1,0:T(8,128)(2,1)}, u32[]{:S(2)}) copy-start(bf16[8,16,8,512]{3,2,1,0:T(8,128)(2,1)} %get-tuple-element.31) | copy-start | bytes 3145732
  129.1 6.0 %copy-start.9 = (bf16[8,128,448]{2,1,0:T(8,128)(2,1)S(1)}, bf16[8,128,448]{2,1,0:T(8,128)(2,1)}, u32[]{:S(2)}) copy-start(bf16[8,128,448]{2,1,0:T(8,128)(2,1)} %get-tuple-element.32) | copy-start | bytes 2752516
  129.1 7.6 %copy-start.6 = (bf16[8,16,8,512]{3,2,1,0:T(8,128)(2,1)S(1)}, bf16[8,16,8,512]{3,2,1,0:T(8,128)(2,1)}, u32[]{:S(2)}) copy-start(bf16[8,16,8,512]{3,2,1,0:T(8,128)(2,1)} %get-tuple-element.35) | copy-start | bytes 3145732
  129.1 7.6 %copy-start.7 = (bf16[8,128,448]{2,1,0:T(8,128)(2,1)S(1)}, bf16[8,128,448]{2,1,0:T(8,128)(2,1)}, u32[]{:S(2)}) copy-start(bf16[8,128,448]{2,1,0:T(8,128)(2,1)} %get-tuple-element.34) | copy-start | bytes 2752516
  135.1 3.3 %copy-start.2 = (bf16[8,4096]{1,0:T(8,128)(2,1)S(1)}, bf16[8,4096]{1,0:T(8,128)(2,1)}, u32[]{:S(2)}) copy-start(bf16[8,4096]{1,0:T(8,128)(2,1)} %get-tuple-element.46) | copy-start | bytes 196612
  135.1 3.9 %copy-start.1 = (bf16[8,4096]{1,0:T(8,128)(2,1)S(1)}, bf16[8,4096]{1,0:T(8,128)(2,1)}, u32[]{:S(2)}) copy-start(bf16[8,4096]{1,0:T(8,128)(2,1)} %get-tuple-element.47) | copy-start | bytes 196612
  135.1 4.5 %copy-start = (bf16[128,256]{1,0:T(8,128)(2,1)S(1)}, bf16[128,256]{1,0:T(8,128)(2,1)}, u32[]{:S(2)}) copy-start(bf16[128,256]{1,0:T(8,128)(2,1)} %get-tuple-element.48) | copy-start | bytes 196612
  135.1 5.1 %copy-start.4 = (f32[8,1024]{1,0:T(8,128)S(1)}, f32[8,1024]{1,0:T(8,128)}, u32[]{:S(2)}) copy-start(f32[8,1024]{1,0:T(8,128)} %get-tuple-element.49) | copy-start | bytes 98308
  135.1 5.8 %copy-start.3 = (f32[8,1024]{1,0:T(8,128)S(1)}, f32[8,1024]{1,0:T(8,128)}, u32[]{:S(2)}) copy-start(f32[8,1024]{1,0:T(8,128)} %get-tuple-element.50) | copy-start | bytes 98308
  135.1 6.4 %copy-start.5 = (f32[1,4096]{1,0:T(1,128)S(1)}, f32[1,4096]{1,0:T(1,128)}, u32[]{:S(2)}) copy-start(f32[1,4096]{1,0:T(1,128)} %get-tuple-element.28) | copy-start | bytes 49156

commit v3 on v2

--- a/solution.py
+++ b/solution.py
@@ -25,10 +25,38 @@
 FAR = [(1, 0), (3, 0), (0, 1), (1, 1), (3, 1), (2, 0), (2, 1)]
 
 
+class Copy:
+    def __init__(self, net, cp):
+        self.net, self.cp = net, cp
+
+    def start(self):
+        self.net.to_send.append(self)
+        self.net.to_recv.append(self)
+        self.cp.start()
+
+    def wait_recv(self):
+        self.net.to_recv = [s for s in self.net.to_recv if s is not self]
+        self.cp.wait_recv()
+
+    def wait_send(self):
+        self.net.to_send = [s for s in self.net.to_send if s is not self]
+        self.cp.wait_send()
+
+
+class Load(Copy):
+    def start(self):
+        self.net.to_recv.append(self)
+        self.cp.start()
+
+    def wait_recv(self):
+        self.net.to_recv = [s for s in self.net.to_recv if s is not self]
+        self.cp.wait()
+
+
 class Net:
     def __init__(self, ssem, rsem):
         self.ssem, self.rsem, self.used = ssem, rsem, 0
-        self.sent = []
+        self.to_send, self.to_recv = [], []
         self.c = lax.axis_index("ctx")
         self.f = lax.axis_index("ffn")
         self.core = lax.rem(self.f, 2)
@@ -46,21 +74,18 @@
             device_id=(self.c if c is None else c, self.f if f is None else f),
             device_id_type=MESH,
         )
-        self.sent.append(cp)
-        return cp
+        return Copy(self, cp)
 
     def local(self, src, dst):
         n = self.used
         self.used = n + 1
-        return pltpu.make_async_copy(src, dst, self.rsem.at[n])
-
-    def done(self, copies):
-        for cp in copies:
+        return Load(self, pltpu.make_async_copy(src, dst, self.rsem.at[n]))
+
+    def drain(self):
+        for cp in list(self.to_recv):
+            cp.wait_recv()
+        for cp in list(self.to_send):
             cp.wait_send()
-            self.sent = [s for s in self.sent if s is not cp]
-
-    def drain(self):
-        self.done(list(self.sent))
 
     def ctx_at(self, d):
         x, y = self.c // 2, lax.rem(self.c, 2)
@@ -106,66 +131,92 @@
     return [net.copy(src, dst.at[net.c], c=net.ctx_at(d)) for d in FAR]
 
 
-class CtxRelay:
-    def __init__(self, net, src, buf):
-        self.net, self.buf = net, buf
-        mine = buf.at[net.c]
-        self.pair = net.copy(src, mine, c=net.ctx_at((0, 1)))
-        self.up = net.copy(src, mine, c=net.ctx_at((1, 0)))
-        self.down = net.copy(src, mine, c=net.ctx_at((3, 0)))
+class Relay:
+    def __init__(self, net, src, slot, at, send, share):
+        self.net, self.slot, self.at, self.send, self.share = net, slot, at, send, share
+        self.near = []
+        mine = slot(at((0, 0)))
+        self.pair = send(src, mine, (0, 1))
+        self.up = send(src, mine, (1, 0))
+        self.down = send(src, mine, (3, 0))
+        if share:
+            self.near.append(net.copy(src, mine, f=net.partner))
 
     def start(self):
-        self.pair.start()
-        self.up.start()
-        self.down.start()
+        start_all([self.pair, self.up, self.down] + self.near)
+
+    def take(self, cp, d):
+        cp.wait_recv()
+        block = self.slot(self.at(d))
+        if self.share:
+            near = self.net.copy(block, block, f=self.net.partner)
+            near.start()
+            self.near.append(near)
+        return block
 
     def pump(self):
-        net, buf = self.net, self.buf
-        self.pair.wait_recv()
-        other = buf.at[net.ctx_at((0, 1))]
-        self.up2 = net.copy(other, other, c=net.ctx_at((1, 0)))
-        self.down2 = net.copy(other, other, c=net.ctx_at((3, 0)))
-        self.up2.start()
-        self.down2.start()
-        self.up.wait_recv()
-        below = buf.at[net.ctx_at((3, 0))]
-        self.up3 = net.copy(below, below, c=net.ctx_at((1, 0)))
+        other = self.take(self.pair, (0, 1))
+        self.up2 = self.send(other, other, (1, 0))
+        self.down2 = self.send(other, other, (3, 0))
+        start_all([self.up2, self.down2])
+        below = self.take(self.up, (3, 0))
+        self.up3 = self.send(below, below, (1, 0))
         self.up3.start()
-        self.down2.wait_recv()
-        above = buf.at[net.ctx_at((1, 1))]
-        self.down3 = net.copy(above, above, c=net.ctx_at((3, 0)))
+        above = self.take(self.down2, (1, 1))
+        self.down3 = self.send(above, above, (3, 0))
         self.down3.start()
 
     def finish(self):
-        wait_all([self.down, self.up2, self.up3, self.down3])
-
-
-class CtxColumns:
-    def __init__(self, net, src, dst):
-        self.net, self.dst = net, dst
-        half = pl.ds(net.core * 8, 8)
-        self.half = half
+        self.take(self.down, (1, 0))
+        self.take(self.up2, (3, 1))
+        self.take(self.up3, (2, 0))
+        self.take(self.down3, (2, 1))
+
+    def close(self):
+        wait_all(self.near)
+
+
+def ctx_relay(net, src, slot):
+    return Relay(
+        net, src, slot, net.ctx_at, lambda s, t, d: net.copy(s, t, c=net.ctx_at(d)), False
+    )
+
+
+def ffn_relay(net, src, slot):
+    def at(d):
+        return net.chip_at(d) * 2 + net.core
+
+    return Relay(net, src, slot, at, lambda s, t, d: net.copy(s, t, f=at(d)), True)
+
+
+class Columns:
+    def __init__(self, net, src, mid, dst):
+        self.net, self.mid, self.dst = net, mid, dst
+        own = pl.ds(pl.multiple_of(net.c * 512, 512), 512)
+        mid[net.c] = src[:, own]
         self.far = []
         for d in FAR:
             to = net.ctx_at(d)
             cols = pl.ds(pl.multiple_of(to * 512, 512), 512)
-            self.far.append(net.copy(src.at[half, :, cols], dst.at[net.c, half], c=to))
+            self.far.append(net.copy(src.at[:, cols], mid.at[net.c], c=to))
 
     def start(self):
         start_all(self.far)
 
-    def forward(self):
-        net = self.net
-        self.near = []
-        for d, cp in zip(FAR, self.far):
-            cp.wait_recv()
-            block = self.dst.at[net.ctx_from(d), self.half]
-            near = net.copy(block, block, f=net.partner)
-            near.start()
-            self.near.append(near)
+    def middle(self):
+        wait_all(self.far)
+        self.dst[:, self.net.f] = self.mid[...]
+        self.relay = ffn_relay(self.net, self.mid, lambda i: self.dst.at[:, i])
+        self.relay.start()
+
+    def pump(self):
+        self.relay.pump()
 
     def finish(self):
-        wait_all(self.near)
+        self.relay.finish()
+
+    def close(self):
+        self.relay.close()
 
 
 class FfnGather:
@@ -248,7 +299,8 @@
         return jnp.concatenate(pieces, axis=1)
 
     def drain(self):
-        self.net.done(self.pair + [cp for far in self.far for cp in far])
+        for cp in self.pair + [cp for far in self.far for cp in far]:
+            cp.wait_send()
 
 
 def seg_starts(doc_ref, pos):
@@ -268,12 +320,22 @@
     return jnp.transpose(jnp.broadcast_to(column, (128, 128)))[0:1, :]
 
 
+def in_rows(blocks):
+    return jnp.concatenate([blocks[i, b] for i in range(CTX) for b in range(16)], axis=0)
+
+
+def flat(blocks):
+    return jnp.concatenate([blocks[b] for b in range(16)], axis=0)
+
+
 def layer(
     keys, values, q, pos, doc, resid, gain, cot, wout_h, wgate_h, wup_h, wdown_h,
-    mixed, gres, dq, kg, vg, gg, nrm_c, cot_c, gres_c, gate_all, up_all, act_all, att_all,
-    wout, wgate, wup, wdown, att, kv_all, q_all, pos_all, nrm_all, cot_all, grows, xr, gact,
+    mixed, gres, dq, kg, vg, gg, dwout_h, dwgate_h, dwup_h, dwdown_h,
+    wout, wgate, wup, wdown, dwout, dwgate, dwup, dwdown, att, kv_all, q_all, pos_all,
+    nrm_all, cot_all, grows, xr, gact,
     part, pair_in, summed, got, part2, pair_in2, summed2, got2,
-    nbuf, gbuf, act, ggate, gup, ga, ga_all, stats, stats_all,
+    nbuf, gbuf, act, ggate, gup, act_t, gate_t, up_t, att_t, act_all, gate_all, up_all, att_all,
+    cot_mid, nrm_mid, gres_mid, cot_c, nrm_c, gres_c, ga, ga_all, stats, stats_all,
     kv, kv_in, gsum, gpair, gchip, gctx_b, gctx, ssem, rsem,
 ):
     net = Net(ssem, rsem)
@@ -290,15 +352,22 @@
     ]
     start_all(loads)
     net.greet()
+
+    def lanes(i):
+        return pl.ds(pl.multiple_of(i * 128, 128), 128)
+
     mine = kv_all.at[net.core, c]
     kv_far = [net.copy(mine, mine, c=net.ctx_at(d)) for d in FAR]
     pos_far = ctx_gather(net, pos, pos_all)
     start_all(kv_far)
     start_all(pos_far)
+    cot_cols = Columns(net, cot, cot_mid, cot_c)
+    cot_cols.start()
+    cot_all[f] = cot[...]
+    cot_ag = ffn_relay(net, cot, lambda i: cot_all.at[i])
+    cot_ag.start()
     q_all[c] = q[...]
-    cot_all[f] = cot[...]
-    cot_ag = FfnGather(net, cot, cot_all)
-    q_ag = CtxRelay(net, q, q_all)
+    q_ag = ctx_relay(net, q, lambda i: q_all.at[i])
     kv_near = []
     for d, cp in zip(FAR, kv_far):
         cp.wait_recv()
@@ -306,12 +375,12 @@
         near = net.copy(block, block, f=net.partner)
         near.start()
         kv_near.append(near)
-    cot_ag.start()
+    cot_ag.pump()
+    q_ag.start()
     wait_all(pos_far)
     wait_all(kv_near)
-    q_ag.start()
-    kpos = jnp.concatenate([pos_all[i] for i in range(CTX)], axis=1)
-    qpos = as_column(pos[...])[:, 0:1]
+    kpos = jnp.concatenate([pos_all[i] for i in range(CTX)], axis=1).astype(F32)
+    qpos = as_column(pos[...].astype(F32))[:, 0:1]
     visible = (kpos <= qpos) & (kpos >= seg_starts(doc, qpos))
     k = kv_all[0].reshape(1024, 128)
     v = kv_all[1].reshape(1024, 128)
@@ -327,24 +396,24 @@
         att[:, hs] = o.astype(BF)
         lcol.append(top + jnp.log(total))
     a = att[...]
-    loads[0].wait()
+    loads[0].wait_recv()
     rs = FfnScatter(net, part, pair_in, summed, got)
     for n in range(CHUNKS):
         rs.put(n, jnp.dot(a, wout[:, n * WIDE : (n + 1) * WIDE], preferred_element_type=F32))
-    att_all[c] = a
-    att_ag = CtxRelay(net, att, att_all)
+    cot_cols.middle()
     for n in range(CHUNKS):
         rs.middle(n)
-    cot_ag.forward()
+    at = jnp.transpose(a.astype(F32)).astype(BF)
+    att_t[...] = at
+    att_all[:, lanes(c)] = at
+    att_ag = ctx_relay(net, att_t, lambda i: att_all.at[:, lanes(i)])
+    att_ag.start()
     q_ag.pump()
-    att_ag.start()
     cot_ag.finish()
-    loads[1].wait()
-    rows = jnp.concatenate([cot_all[b] for b in range(16)], axis=0)
-    gact[...] = lax.dot_general(rows, wdown[...], NT, preferred_element_type=F32)
-    own = pl.ds(pl.multiple_of(c * 512, 512), 512)
-    cot_c[c] = cot_all[:, :, own]
-    cot_cols = CtxColumns(net, cot_all, cot_c)
+    cot_cols.pump()
+    cot_ag.close()
+    loads[1].wait_recv()
+    gact[...] = lax.dot_general(flat(cot_all), wdown[...], NT, preferred_element_type=F32)
     projected = rs.finish()
     hidden = (resid[...].astype(F32) + projected).astype(BF)
     hf = hidden.astype(F32)
@@ -354,18 +423,19 @@
     nrm_all[f] = normed
     ag = FfnGather(net, nbuf, nrm_all)
     ag.start()
-    cot_cols.start()
+    nrm_cols = Columns(net, nbuf, nrm_mid, nrm_c)
+    nrm_cols.start()
+    att_ag.pump()
+    cot_cols.finish()
+    rs.drain()
     ag.forward()
-    att_ag.pump()
     ag.finish()
-    nrm_cols = CtxColumns(net, nrm_all, nrm_c)
-    nrm_cols.start()
-    nrm_c[c] = nrm_all[:, :, own]
-    xr[...] = jnp.concatenate([nrm_all[b] for b in range(16)], axis=0)
-    loads[2].wait()
-    gate_pre = jnp.dot(xr[...], wgate[...], preferred_element_type=F32)
-    loads[3].wait()
-    up_proj = jnp.dot(xr[...], wup[...], preferred_element_type=F32)
+    nrm_cols.middle()
+    xr[...] = flat(nrm_all)
+    loads[2].wait_recv()
+    gate_pre = lax.dot_general(xr[...], wgate[...], NT, preferred_element_type=F32)
+    loads[3].wait_recv()
+    up_proj = lax.dot_general(xr[...], wup[...], NT, preferred_element_type=F32)
     sig = jax.nn.sigmoid(gate_pre)
     grad_act = gact[...]
     activated = (gate_pre * sig * up_proj).astype(BF)
@@ -374,34 +444,33 @@
     act[...] = activated
     ggate[...] = grad_gate
     gup[...] = grad_up
-    rs.drain()
     rs = FfnScatter(net, part, pair_in, summed, got)
     for n in range(CHUNKS):
         span = slice(n * WIDE, (n + 1) * WIDE)
         rs.put(
             n,
-            lax.dot_general(ggate[...], wgate[span, :], NT, preferred_element_type=F32)
-            + lax.dot_general(gup[...], wup[span, :], NT, preferred_element_type=F32),
+            jnp.dot(ggate[...], wgate[:, span], preferred_element_type=F32)
+            + jnp.dot(gup[...], wup[:, span], preferred_element_type=F32),
         )
-    gate_all[c] = ggate[...]
-    up_all[c] = gup[...]
-    act_all[c] = act[...]
-    gate_ag = CtxRelay(net, ggate, gate_all)
-    up_ag = CtxRelay(net, gup, up_all)
-    act_ag = CtxRelay(net, act, act_all)
-    gate_ag.start()
-    up_ag.start()
-    act_ag.start()
-    for n in range(CHUNKS):
-        rs.middle(n)
-    cot_cols.forward()
-    nrm_cols.forward()
+    relays = []
+    for src, turned, gathered in ((ggate, gate_t, gate_all), (gup, up_t, up_all), (act, act_t, act_all)):
+        turn = jnp.transpose(src[...].astype(F32)).astype(BF)
+        turned[...] = turn
+        gathered[:, lanes(c)] = turn
+        relay = ctx_relay(net, turned, lambda i, gathered=gathered: gathered.at[:, lanes(i)])
+        relay.start()
+        relays.append(relay)
+        if len(relays) <= CHUNKS:
+            rs.middle(len(relays) - 1)
+    gate_ag, up_ag, act_ag = relays
+    nrm_cols.pump()
     rs2 = FfnScatter(net, part2, pair_in2, summed2, got2)
     for n in range(CHUNKS):
         rs2.put(
             n, jnp.dot(act[...], wdown[:, n * WIDE : (n + 1) * WIDE], preferred_element_type=F32)
         )
     gate_ag.pump()
+    att_ag.finish()
     gnorm = rs.finish()
     gained = gnorm * gain[...]
     cube = ir * ir * ir
@@ -413,9 +482,12 @@
     gsum[...] = jnp.sum(gnorm * hf * ir, axis=0, keepdims=True)
     ag = FfnGather(net, gbuf, grows)
     ag.start()
+    gres_cols = Columns(net, gbuf, gres_mid, gres_c)
+    gres_cols.start()
     g1 = net.copy(gsum, gpair, f=net.partner)
     g1.start()
     up_ag.pump()
+    nrm_cols.finish()
     g1.wait_recv()
     gchip[net.chip] = gsum[...] + gpair[...]
     g2 = [
@@ -423,15 +495,13 @@
         for d in FAR
     ]
     start_all(g2)
+    act_ag.pump()
     ag.forward()
     ag.finish()
-    for n in range(CHUNKS):
-        rs2.middle(n)
-    rows = jnp.concatenate([grows[b] for b in range(16)], axis=0)
-    gat = lax.dot_general(rows, wout[...], NT, preferred_element_type=F32).astype(BF)
+    gat = lax.dot_general(flat(grows), wout[...], NT, preferred_element_type=F32).astype(BF)
     ga[...] = gat
     ga_all[c] = gat
-    prod = gat.astype(F32) * att[...].astype(F32)
+    prod = gat.astype(F32) * a.astype(F32)
     delta = [jnp.sum(prod[:, h * 128 : (h + 1) * 128], axis=1, keepdims=True) for h in range(2)]
     st = jnp.concatenate(
         [as_row(r) for r in lcol + delta] + [jnp.zeros((4, 128), F32)], axis=0
@@ -440,10 +510,9 @@
     stats_all[c] = st
     late = ctx_gather(net, ga, ga_all) + ctx_gather(net, stats, stats_all)
     start_all(late)
-    gres_cols = CtxColumns(net, grows, gres_c)
-    gres_cols.start()
-    gres_c[c] = grows[:, :, own]
-    act_ag.pump()
+    gres_cols.middle()
+    for n in range(CHUNKS):
+        rs2.middle(n)
     k = kv_all[0].reshape(1024, 128)
     v = kv_all[1].reshape(1024, 128)
     for h in range(2):
@@ -461,6 +530,21 @@
     gctx[c] = tot
     g3 = ctx_gather(net, gctx_b, gctx)
     start_all(g3)
+    gres_cols.pump()
+    nrm_cols.close()
+    gate_ag.finish()
+    up_ag.finish()
+    rows = in_rows(nrm_c)
+    stores = []
+
+    def weight_gradient(left, right, buf, out):
+        buf[...] = jnp.dot(left[...], right, preferred_element_type=F32)
+        store = net.local(buf, out)
+        store.start()
+        stores.append(store)
+
+    weight_gradient(gate_all, rows, dwgate, dwgate_h)
+    weight_gradient(up_all, rows, dwup, dwup_h)
     q_ag.finish()
     wait_all(late)
     vis_t = (qpos <= kpos) & (qpos >= seg_starts(doc, kpos))
@@ -489,8 +573,13 @@
         to = lax.rem(f + n, 16)
         last.append(net.copy(kv.at[to], kv_in.at[f], f=to))
     start_all(last)
-    gres_cols.forward()
+    gres_cols.finish()
     mixed[...] = (hf + rs2.finish()).astype(BF)
+    act_ag.finish()
+    cot_cols.close()
+    weight_gradient(act_all, in_rows(cot_c), dwdown, dwdown_h)
+    gres_cols.close()
+    weight_gradient(att_all, in_rows(gres_c), dwout, dwout_h)
     wait_all(g3)
     tot = gctx[0]
     for i in range(1, CTX):
@@ -501,9 +590,20 @@
         pair = kv_in[2 * g] + kv_in[2 * g + 1]
         kg[:, g * 128 : (g + 1) * 128] = pair[:, 0:128]
         vg[:, g * 128 : (g + 1) * 128] = pair[:, 128:256]
-    for gather in (cot_cols, nrm_cols, gres_cols, gate_ag, up_ag, act_ag, att_ag):
-        gather.finish()
+    wait_all(stores)
     net.drain()
+
+
+def hand_over(*refs):
+    n = (len(refs) - 1) // 2
+    sems = refs[-1]
+    copies = [
+        pltpu.make_async_copy(refs[i], refs[n + i], sems.at[i]) for i in range(n)
+    ]
+    for cp in copies:
+        cp.start()
+    for cp in copies:
+        cp.wait()
 
 
 VM = pl.BlockSpec(memory_space=pltpu.VMEM)
@@ -515,88 +615,78 @@
     resid_in, queries, keys_in, value_rows_input, w_out, norm_gain, w_gate, w_up, w_down,
     cotangent, positions, doc_ids,
 ):
-    pos = positions.astype(F32).reshape(1, 128)
-    doc = doc_ids.reshape(8, 128)
-    gain = norm_gain.reshape(1, 4096)
-    outs = [
+    small = [
         ((8, 4096), BF),
         ((8, 4096), BF),
         ((128, 256), BF),
         ((8, 1024), F32),
         ((8, 1024), F32),
         ((1, 4096), F32),
-        ((8, 16, 8, 512), BF),
-        ((8, 16, 8, 512), BF),
-        ((8, 16, 8, 512), BF),
-        ((8, 128, 448), BF),
-        ((8, 128, 448), BF),
-        ((8, 128, 448), BF),
-        ((8, 128, 256), BF),
     ]
-    scratch = [
-        ((256, 4096), BF),
-        ((4096, 448), BF),
-        ((4096, 448), BF),
-        ((448, 4096), BF),
-        ((128, 256), BF),
-        ((2, 8, 128, 128), BF),
-        ((8, 128, 256), BF),
-        ((8, 1, 128), F32),
-        ((16, 8, 4096), BF),
-        ((16, 8, 4096), BF),
-        ((16, 8, 4096), BF),
-        ((128, 4096), BF),
-        ((128, 448), F32),
-    ]
-    scratch += [((8, 2, 8, 4096), BF)] + [((8, 8, 4096), BF)] * 3
-    scratch += [((8, 2, 8, 4096), BF)] + [((8, 8, 4096), BF)] * 3
-    scratch += [
-        ((8, 4096), BF),
-        ((8, 4096), BF),
-        ((128, 448), BF),
-        ((128, 448), BF),
-        ((128, 448), BF),
-        ((128, 256), BF),
-        ((8, 128, 256), BF),
-        ((8, 128), F32),
-        ((8, 8, 128), F32),
-        ((16, 8, 256), F32),
-        ((16, 8, 256), F32),
-        ((1, 4096), F32),
-        ((1, 4096), F32),
-        ((8, 1, 4096), F32),
-        ((1, 4096), F32),
-        ((8, 1, 4096), F32),
-    ]
-    (mixed, gres, dq, kg, vg, gg, nrm_c, cot_c, gres_c, gate_all, up_all, act_all, att_all) = (
-        pl.pallas_call(
-            layer,
-            out_shape=[jax.ShapeDtypeStruct(s, d) for s, d in outs],
-            in_specs=[VM] * 8 + [ANY] * 4,
-            out_specs=[VM] * len(outs),
-            scratch_shapes=[pltpu.VMEM(s, d) for s, d in scratch]
-            + [pltpu.SemaphoreType.DMA((SEMS,)), pltpu.SemaphoreType.DMA((SEMS,))],
-            compiler_params=pltpu.CompilerParams(
-                collective_id=0, has_side_effects=True, vmem_limit_bytes=60 * 2**20
-            ),
-        )(
-            keys_in, value_rows_input, queries, pos, doc, resid_in, gain, cotangent,
-            w_out, w_gate, w_up, w_down,
-        )
+    grads = [((256, 512), F32)] + [((448, 512), F32)] * 3
+    shard = [((8, 2, 8, 4096), BF)] + [((8, 8, 4096), BF)] * 3
+    scratch = (
+        [((256, 4096), BF)]
+        + [((448, 4096), BF)] * 3
+        + grads
+        + [
+            ((128, 256), BF),
+            ((2, 8, 128, 128), BF),
+            ((8, 128, 256), BF),
+            ((8, 1, 128), jnp.int32),
+            ((16, 8, 4096), BF),
+            ((16, 8, 4096), BF),
+            ((16, 8, 4096), BF),
+            ((128, 4096), BF),
+            ((128, 448), F32),
+        ]
+        + shard
+        + shard
+        + [((8, 4096), BF)] * 2
+        + [((128, 448), BF)] * 3
+        + [((448, 128), BF)] * 3
+        + [((256, 128), BF)]
+        + [((448, 1024), BF)] * 3
+        + [((256, 1024), BF)]
+        + [((8, 8, 512), BF)] * 3
+        + [((8, 16, 8, 512), BF)] * 3
+        + [
+            ((128, 256), BF),
+            ((8, 128, 256), BF),
+            ((8, 128), F32),
+            ((8, 8, 128), F32),
+            ((16, 8, 256), F32),
+            ((16, 8, 256), F32),
+            ((1, 4096), F32),
+            ((1, 4096), F32),
+            ((8, 1, 4096), F32),
+            ((1, 4096), F32),
+            ((8, 1, 4096), F32),
+        ]
     )
-    contract = functools.partial(
-        lax.dot_general,
-        dimension_numbers=(((0,), (0,)), ((), ())),
-        preferred_element_type=F32,
+    shapes = [jax.ShapeDtypeStruct(s, d) for s, d in small + grads]
+    results = pl.pallas_call(
+        layer,
+        out_shape=shapes,
+        in_specs=[VM] * 8 + [ANY] * 4,
+        out_specs=[VM] * len(small) + [ANY] * len(grads),
+        scratch_shapes=[pltpu.VMEM(s, d) for s, d in scratch]
+        + [pltpu.SemaphoreType.DMA((SEMS,)), pltpu.SemaphoreType.DMA((SEMS,))],
+        compiler_params=pltpu.CompilerParams(
+            collective_id=0, has_side_effects=True, vmem_limit_bytes=60 * 2**20
+        ),
+    )(
+        keys_in, value_rows_input, queries, positions.reshape(1, 128), doc_ids.reshape(8, 128),
+        resid_in, norm_gain.reshape(1, 4096), cotangent, w_out, w_gate.T, w_up.T, w_down,
     )
-    nrm_c = nrm_c.reshape(1024, 512)
-    grad_w_out = contract(att_all.reshape(1024, 256), gres_c.reshape(1024, 512))
-    grad_w_gate = contract(nrm_c, gate_all.reshape(1024, 448))
-    grad_w_up = contract(nrm_c, up_all.reshape(1024, 448))
-    grad_w_down = contract(act_all.reshape(1024, 448), cot_c.reshape(1024, 512))
-    return (
-        mixed, gres, dq, kg, vg, gg.reshape(4096), grad_w_out, grad_w_gate, grad_w_up, grad_w_down,
-    )
+    mixed, gres, dq, kg, vg, gg, dwout, dwgate, dwup, dwdown = pl.pallas_call(
+        hand_over,
+        out_shape=shapes,
+        in_specs=[VM] * len(shapes),
+        out_specs=[ANY] * len(shapes),
+        scratch_shapes=[pltpu.SemaphoreType.DMA((len(shapes),))],
+    )(*results)
+    return (mixed, gres, dq, kg, vg, gg.reshape(4096), dwout, dwgate.T, dwup.T, dwdown)
 
 
 def solution(mesh):

time: 142 us -> 114 us (0.80)
  local copies, waits for them, and re-layouts: 16.6 us -> 0 us
  matrix products: 9.14 us -> 0 us
  Pallas kernels: 114 us -> 112 us
    unnamed x28 -> x0, local copies, waits for them, and re-layouts: 16.6 us -> none
    dot_general x4 -> x0, matrix products: 9.14 us -> none  [the longest x1 3.15 us: body(): grad_w_up = contract(nrm_c, up_all.reshape(1024, 448))]
    pallas_call x1 -> x2, Pallas kernels: 114 us -> 112 us  [the longest x1 108 us: body(): pl.pallas_call(layer, out_shape=shapes, in_specs=[VM] * 8 + [ANY] * 4, ou...]
where the time goes in v3:
time: 114 us; the launch traced here: 113 us
  Pallas kernels  112 us (98%)
    pallas_call x1, Pallas kernels, body(): pl.pallas_call(layer, out_shape=shapes, in_specs=[VM] * 8 + [ANY] * 4, ou...  108 us
    pallas_call x1, Pallas kernels, body(): pl.pallas_call(hand_over, out_shape=shapes, in_specs=[VM] * len(shapes),...  3.91 us

profile of v3, /device:TPU:1, one launch (start us, length us, event | category | flops | bytes accessed | tf_op | source)
XLA Modules:
  0.0 112.9 jit_solution(3673852622494803327)
XLA Ops:
  0.6 108.1 %shard_map.195 = (bf16[8,4096]{1,0:T(8,128)(2,1)}, bf16[8,4096]{1,0:T(8,128)(2,1)}, bf16[128,256]{1,0:T(8,128)(2,1)}, f32[8,1024]{1,0:T(8,128)}, f32[8,1024]{1,0...) custom-call(bf16[128,1024]{1,0:T(8,128)(2,1)} %keys.1, ...), custom_call_target="tpu_custom_call" | custom-call | tf_op jit(solution)/shard_map/pallas_call | solution.py:668
  108.8 3.9 %shard_map.196 = (bf16[8,4096]{1,0:T(8,128)(2,1)}, bf16[8,4096]{1,0:T(8,128)(2,1)}, bf16[128,256]{1,0:T(8,128)(2,1)}, f32[8,1024]{1,0:T(8,128)}, f32[8,1024]{1,0...) custom-call(bf16[8,4096]{1,0:T(8,128)(2,1)} %get-tuple-element.30.re, ...), custom_call_target="tpu_custom_call" | custom-call | tf_op jit(solution)/shard_map/pallas_call | solution.py:682

commit v4 on v3

--- a/solution.py
+++ b/solution.py
@@ -22,7 +22,7 @@
 
 CHUNKS = 2
 WIDE = 4096 // CHUNKS
-FAR = [(1, 0), (3, 0), (0, 1), (1, 1), (3, 1), (2, 0), (2, 1)]
+FAR = [(2, 1), (2, 0), (1, 1), (3, 1), (0, 1), (1, 0), (3, 0)]
 
 
 class Copy:
@@ -114,7 +114,10 @@
                 device_id=(self.c, lax.rem(self.f + k, 16)),
                 device_id_type=MESH,
             )
-        pl.semaphore_wait(barrier, 22)
+        self.barrier = barrier
+
+    def met(self):
+        pl.semaphore_wait(self.barrier, 22)
 
 
 def start_all(copies):
@@ -143,7 +146,14 @@
             self.near.append(net.copy(src, mine, f=net.partner))
 
     def start(self):
-        start_all([self.pair, self.up, self.down] + self.near)
+        self.start_pair()
+        self.start_ring()
+
+    def start_pair(self):
+        start_all([self.pair] + self.near)
+
+    def start_ring(self):
+        start_all([self.up, self.down])
 
     def take(self, cp, d):
         cp.wait_recv()
@@ -162,6 +172,8 @@
         below = self.take(self.up, (3, 0))
         self.up3 = self.send(below, below, (1, 0))
         self.up3.start()
+
+    def pump2(self):
         above = self.take(self.down2, (1, 1))
         self.down3 = self.send(above, above, (3, 0))
         self.down3.start()
@@ -203,6 +215,12 @@
     def start(self):
         start_all(self.far)
 
+    def direct(self):
+        wait_all(self.far)
+        self.dst[:, self.net.f] = self.mid[...]
+        self.gather = FfnGather(self.net, self.mid, lambda i: self.dst.at[:, i])
+        self.gather.start()
+
     def middle(self):
         wait_all(self.far)
         self.dst[:, self.net.f] = self.mid[...]
@@ -212,6 +230,9 @@
     def pump(self):
         self.relay.pump()
 
+    def pump2(self):
+        self.relay.pump2()
+
     def finish(self):
         self.relay.finish()
 
@@ -220,10 +241,11 @@
 
 
 class FfnGather:
-    def __init__(self, net, src, dst):
-        self.net, self.dst = net, dst
-        self.far = [net.copy(src, dst.at[net.f], f=net.chip_at(d) * 2 + net.core) for d in FAR]
-        self.near = [net.copy(src, dst.at[net.f], f=net.partner)]
+    def __init__(self, net, src, slot):
+        self.net, self.slot = net, slot
+        mine = slot(net.f)
+        self.far = [net.copy(src, mine, f=net.chip_at(d) * 2 + net.core) for d in FAR]
+        self.near = [net.copy(src, mine, f=net.partner)]
 
     def start(self):
         start_all(self.far)
@@ -233,7 +255,7 @@
         net = self.net
         for d, cp in zip(FAR, self.far):
             cp.wait_recv()
-            block = self.dst.at[net.chip_from(d) * 2 + net.core]
+            block = self.slot(net.chip_from(d) * 2 + net.core)
             near = net.copy(block, block, f=net.partner)
             near.start()
             self.near.append(near)
@@ -303,6 +325,55 @@
             cp.wait_send()
 
 
+class RingScatter(FfnScatter):
+    def __init__(self, net, part, pair_in, summed, ring_in, half, half_in):
+        self.net, self.part, self.pair_in, self.summed = net, part, pair_in, summed
+        self.ring_in, self.half, self.half_in = ring_in, half, half_in
+        self.pair = [
+            net.copy(
+                part.at[:, 1 - net.core, :, pl.ds(n * WIDE, WIDE)],
+                pair_in.at[:, :, pl.ds(n * WIDE, WIDE)],
+                f=net.partner,
+            )
+            for n in range(CHUNKS)
+        ]
+
+    def middle(self):
+        net = self.net
+        wait_all(self.pair)
+        for chip in range(CHIPS):
+            self.summed[chip] = (
+                self.part[chip, net.core].astype(F32) + self.pair_in[chip].astype(F32)
+            ).astype(BF)
+        self.ring = []
+        for step in (1, 3, 2):
+            to = net.chip_at((step, 0))
+            block = self.summed.at[pl.ds(to // 2 * 2, 2)]
+            cp = net.copy(block, self.ring_in.at[net.chip // 2], f=to * 2 + net.core)
+            cp.start()
+            self.ring.append(cp)
+
+    def middle2(self):
+        net = self.net
+        wait_all(self.ring)
+        z, y = net.chip // 2, lax.rem(net.chip, 2)
+
+        def ring_sum(yh):
+            total = self.summed[z * 2 + yh].astype(F32)
+            for step in (1, 3, 2):
+                total = total + self.ring_in[lax.rem(z + step, 4), yh].astype(F32)
+            return total
+
+        self.half[...] = ring_sum(1 - y).astype(BF)
+        self.across = net.copy(self.half, self.half_in, f=net.chip_at((0, 1)) * 2 + net.core)
+        self.across.start()
+        self.own = ring_sum(y)
+
+    def finish(self):
+        self.across.wait_recv()
+        return self.own + self.half_in[...].astype(F32)
+
+
 def seg_starts(doc_ref, pos):
     doc = doc_ref[...]
     start = jnp.zeros_like(pos)
@@ -329,11 +400,12 @@
 
 
 def layer(
-    keys, values, q, pos, doc, resid, gain, cot, wout_h, wgate_h, wup_h, wdown_h,
-    mixed, gres, dq, kg, vg, gg, dwout_h, dwgate_h, dwup_h, dwdown_h,
+    keys_h, values_h, q_h, pos_h, doc_h, resid_h, gain_h, cot_h, wout_h, wgate_h, wup_h, wdown_h,
+    mixed_h, gres_h, dq_h, kg_h, vg_h, gg_h, dwout_h, dwgate_h, dwup_h, dwdown_h,
+    q, pos, doc, resid, gain, cot, mixed, gres, dq, kg, vg, gg,
     wout, wgate, wup, wdown, dwout, dwgate, dwup, dwdown, att, kv_all, q_all, pos_all,
     nrm_all, cot_all, grows, xr, gact,
-    part, pair_in, summed, got, part2, pair_in2, summed2, got2,
+    part, pair_in, summed, got, part2, pair_in2, summed2, ring_in, half, half_in,
     nbuf, gbuf, act, ggate, gup, act_t, gate_t, up_t, att_t, act_all, gate_all, up_all, att_all,
     cot_mid, nrm_mid, gres_mid, cot_c, nrm_c, gres_c, ga, ga_all, stats, stats_all,
     kv, kv_in, gsum, gpair, gchip, gctx_b, gctx, ssem, rsem,
@@ -341,9 +413,25 @@
     net = Net(ssem, rsem)
     c, f = net.c, net.f
     cols = pl.ds(pl.multiple_of(net.chip * 128, 128), 128)
-    kv_all[0, c] = keys[:, cols]
-    kv_all[1, c] = values[:, cols]
-    pos_all[c] = pos[...]
+    net.greet()
+    stores = []
+
+    def put_out(buf, out):
+        store = net.local(buf, out)
+        store.start()
+        stores.append(store)
+
+    first = [
+        net.local(keys_h.at[:, cols], kv_all.at[0, c]),
+        net.local(values_h.at[:, cols], kv_all.at[1, c]),
+        net.local(pos_h, pos),
+        net.local(cot_h, cot),
+        net.local(q_h, q),
+        net.local(doc_h, doc),
+        net.local(resid_h, resid),
+        net.local(gain_h, gain),
+    ]
+    start_all(first)
     loads = [
         net.local(wout_h, wout),
         net.local(wdown_h, wdown),
@@ -351,7 +439,9 @@
         net.local(wup_h, wup),
     ]
     start_all(loads)
-    net.greet()
+    wait_all(first)
+    pos_all[c] = pos[...]
+    net.met()
 
     def lanes(i):
         return pl.ds(pl.multiple_of(i * 128, 128), 128)
@@ -376,7 +466,6 @@
         near.start()
         kv_near.append(near)
     cot_ag.pump()
-    q_ag.start()
     wait_all(pos_far)
     wait_all(kv_near)
     kpos = jnp.concatenate([pos_all[i] for i in range(CTX)], axis=1).astype(F32)
@@ -395,22 +484,22 @@
         o = jnp.dot(w.astype(BF), v, preferred_element_type=F32) / total
         att[:, hs] = o.astype(BF)
         lcol.append(top + jnp.log(total))
+    cot_ag.pump2()
+    q_ag.start()
     a = att[...]
     loads[0].wait_recv()
     rs = FfnScatter(net, part, pair_in, summed, got)
     for n in range(CHUNKS):
         rs.put(n, jnp.dot(a, wout[:, n * WIDE : (n + 1) * WIDE], preferred_element_type=F32))
-    cot_cols.middle()
     for n in range(CHUNKS):
         rs.middle(n)
+    cot_cols.middle()
     at = jnp.transpose(a.astype(F32)).astype(BF)
     att_t[...] = at
     att_all[:, lanes(c)] = at
     att_ag = ctx_relay(net, att_t, lambda i: att_all.at[:, lanes(i)])
     att_ag.start()
-    q_ag.pump()
     cot_ag.finish()
-    cot_cols.pump()
     cot_ag.close()
     loads[1].wait_recv()
     gact[...] = lax.dot_general(flat(cot_all), wdown[...], NT, preferred_element_type=F32)
@@ -421,15 +510,19 @@
     normed = (hf * ir * gain[...]).astype(BF)
     nbuf[...] = normed
     nrm_all[f] = normed
-    ag = FfnGather(net, nbuf, nrm_all)
+    ag = FfnGather(net, nbuf, lambda i: nrm_all.at[i])
     ag.start()
     nrm_cols = Columns(net, nbuf, nrm_mid, nrm_c)
     nrm_cols.start()
+    q_ag.pump()
+    cot_cols.pump()
     att_ag.pump()
-    cot_cols.finish()
     rs.drain()
     ag.forward()
     ag.finish()
+    q_ag.pump2()
+    cot_cols.pump2()
+    att_ag.pump2()
     nrm_cols.middle()
     xr[...] = flat(nrm_all)
     loads[2].wait_recv()
@@ -444,6 +537,16 @@
     act[...] = activated
     ggate[...] = grad_gate
     gup[...] = grad_up
+    def turned_relay(src, turned, gathered):
+        turn = jnp.transpose(src[...].astype(F32)).astype(BF)
+        turned[...] = turn
+        gathered[:, lanes(c)] = turn
+        return ctx_relay(net, turned, lambda i: gathered.at[:, lanes(i)])
+
+    act_ag = turned_relay(act, act_t, act_all)
+    act_ag.start()
+    gate_ag = turned_relay(ggate, gate_t, gate_all)
+    gate_ag.start()
     rs = FfnScatter(net, part, pair_in, summed, got)
     for n in range(CHUNKS):
         span = slice(n * WIDE, (n + 1) * WIDE)
@@ -452,42 +555,37 @@
             jnp.dot(ggate[...], wgate[:, span], preferred_element_type=F32)
             + jnp.dot(gup[...], wup[:, span], preferred_element_type=F32),
         )
-    relays = []
-    for src, turned, gathered in ((ggate, gate_t, gate_all), (gup, up_t, up_all), (act, act_t, act_all)):
-        turn = jnp.transpose(src[...].astype(F32)).astype(BF)
-        turned[...] = turn
-        gathered[:, lanes(c)] = turn
-        relay = ctx_relay(net, turned, lambda i, gathered=gathered: gathered.at[:, lanes(i)])
-        relay.start()
-        relays.append(relay)
-        if len(relays) <= CHUNKS:
-            rs.middle(len(relays) - 1)
-    gate_ag, up_ag, act_ag = relays
+    up_ag = turned_relay(gup, up_t, up_all)
+    up_ag.start_ring()
+    for n in range(CHUNKS):
+        rs.middle(n)
     nrm_cols.pump()
-    rs2 = FfnScatter(net, part2, pair_in2, summed2, got2)
+    rs2 = RingScatter(net, part2, pair_in2, summed2, ring_in, half, half_in)
     for n in range(CHUNKS):
         rs2.put(
             n, jnp.dot(act[...], wdown[:, n * WIDE : (n + 1) * WIDE], preferred_element_type=F32)
         )
-    gate_ag.pump()
+    cot_cols.finish()
     att_ag.finish()
+    q_ag.finish()
     gnorm = rs.finish()
     gained = gnorm * gain[...]
     cube = ir * ir * ir
     mean = jnp.mean(gained * hf, axis=1, keepdims=True)
     gr = (cot[...].astype(F32) + ir * gained - hf * cube * mean).astype(BF)
     gres[...] = gr
+    put_out(gres, gres_h)
     gbuf[...] = gr
     grows[f] = gr
     gsum[...] = jnp.sum(gnorm * hf * ir, axis=0, keepdims=True)
-    ag = FfnGather(net, gbuf, grows)
+    ag = FfnGather(net, gbuf, lambda i: grows.at[i])
     ag.start()
     gres_cols = Columns(net, gbuf, gres_mid, gres_c)
     gres_cols.start()
     g1 = net.copy(gsum, gpair, f=net.partner)
     g1.start()
-    up_ag.pump()
-    nrm_cols.finish()
+    up_ag.start_pair()
+    rs2.middle()
     g1.wait_recv()
     gchip[net.chip] = gsum[...] + gpair[...]
     g2 = [
@@ -496,6 +594,8 @@
     ]
     start_all(g2)
     act_ag.pump()
+    gate_ag.pump()
+    nrm_cols.pump2()
     ag.forward()
     ag.finish()
     gat = lax.dot_general(flat(grows), wout[...], NT, preferred_element_type=F32).astype(BF)
@@ -510,9 +610,12 @@
     stats_all[c] = st
     late = ctx_gather(net, ga, ga_all) + ctx_gather(net, stats, stats_all)
     start_all(late)
-    gres_cols.middle()
-    for n in range(CHUNKS):
-        rs2.middle(n)
+    up_ag.pump()
+    act_ag.pump2()
+    gate_ag.pump2()
+    rs2.middle2()
+    gres_cols.direct()
+    up_ag.pump2()
     k = kv_all[0].reshape(1024, 128)
     v = kv_all[1].reshape(1024, 128)
     for h in range(2):
@@ -522,6 +625,7 @@
         dp = lax.dot_general(ga[:, hs], v, NT, preferred_element_type=F32)
         ds = (p * (dp - delta[h])).astype(BF)
         dq[:, hs] = (jnp.dot(ds, k, preferred_element_type=F32) * SCALE).astype(BF)
+    put_out(dq, dq_h)
     wait_all(g2)
     tot = gchip[0]
     for i in range(1, CHIPS):
@@ -530,22 +634,14 @@
     gctx[c] = tot
     g3 = ctx_gather(net, gctx_b, gctx)
     start_all(g3)
-    gres_cols.pump()
-    nrm_cols.close()
-    gate_ag.finish()
-    up_ag.finish()
-    rows = in_rows(nrm_c)
-    stores = []
 
     def weight_gradient(left, right, buf, out):
         buf[...] = jnp.dot(left[...], right, preferred_element_type=F32)
-        store = net.local(buf, out)
-        store.start()
-        stores.append(store)
-
-    weight_gradient(gate_all, rows, dwgate, dwgate_h)
-    weight_gradient(up_all, rows, dwup, dwup_h)
-    q_ag.finish()
+        put_out(buf, out)
+
+    cot_cols.close()
+    act_ag.finish()
+    weight_gradient(act_all, in_rows(cot_c), dwdown, dwdown_h)
     wait_all(late)
     vis_t = (qpos <= kpos) & (qpos >= seg_starts(doc, kpos))
     k_own = kv_all[0, c]
@@ -573,40 +669,49 @@
         to = lax.rem(f + n, 16)
         last.append(net.copy(kv.at[to], kv_in.at[f], f=to))
     start_all(last)
-    gres_cols.finish()
+    gres_cols.gather.forward()
     mixed[...] = (hf + rs2.finish()).astype(BF)
-    act_ag.finish()
-    cot_cols.close()
-    weight_gradient(act_all, in_rows(cot_c), dwdown, dwdown_h)
-    gres_cols.close()
+    put_out(mixed, mixed_h)
+    gres_cols.gather.finish()
+    nrm_cols.finish()
+    gate_ag.finish()
+    nrm_cols.close()
+    rows = in_rows(nrm_c)
+    weight_gradient(gate_all, rows, dwgate, dwgate_h)
+    up_ag.finish()
+    weight_gradient(up_all, rows, dwup, dwup_h)
     weight_gradient(att_all, in_rows(gres_c), dwout, dwout_h)
     wait_all(g3)
     tot = gctx[0]
     for i in range(1, CTX):
         tot = tot + gctx[i]
     gg[...] = tot
+    put_out(gg, gg_h)
     wait_all(last)
     for g in range(8):
         pair = kv_in[2 * g] + kv_in[2 * g + 1]
         kg[:, g * 128 : (g + 1) * 128] = pair[:, 0:128]
         vg[:, g * 128 : (g + 1) * 128] = pair[:, 128:256]
+    put_out(kg, kg_h)
+    put_out(vg, vg_h)
     wait_all(stores)
     net.drain()
 
 
 def hand_over(*refs):
-    n = (len(refs) - 1) // 2
-    sems = refs[-1]
-    copies = [
-        pltpu.make_async_copy(refs[i], refs[n + i], sems.at[i]) for i in range(n)
-    ]
-    for cp in copies:
+    n = (len(refs) - 2) // 3
+    held, came, left = refs[2 * n : 3 * n], refs[-2], refs[-1]
+    ins = [pltpu.make_async_copy(refs[i], held[i], came.at[i]) for i in range(n)]
+    outs = [pltpu.make_async_copy(held[i], refs[n + i], left.at[i]) for i in range(n)]
+    for cp in ins:
         cp.start()
-    for cp in copies:
+    for cp, out in zip(ins, outs):
         cp.wait()
-
-
-VM = pl.BlockSpec(memory_space=pltpu.VMEM)
+        out.start()
+    for out in outs:
+        out.wait()
+
+
 ANY = pl.BlockSpec(memory_space=pl.ANY)
 SEMS = 320
 
@@ -626,7 +731,10 @@
     grads = [((256, 512), F32)] + [((448, 512), F32)] * 3
     shard = [((8, 2, 8, 4096), BF)] + [((8, 8, 4096), BF)] * 3
     scratch = (
-        [((256, 4096), BF)]
+        [((128, 256), BF), ((1, 128), jnp.int32), ((8, 128), jnp.int32)]
+        + [((8, 4096), BF), ((1, 4096), F32), ((8, 4096), BF)]
+        + small
+        + [((256, 4096), BF)]
         + [((448, 4096), BF)] * 3
         + grads
         + [
@@ -641,7 +749,8 @@
             ((128, 448), F32),
         ]
         + shard
-        + shard
+        + shard[:3]
+        + [((4, 2, 8, 4096), BF), ((8, 4096), BF), ((8, 4096), BF)]
         + [((8, 4096), BF)] * 2
         + [((128, 448), BF)] * 3
         + [((448, 128), BF)] * 3
@@ -668,8 +777,8 @@
     results = pl.pallas_call(
         layer,
         out_shape=shapes,
-        in_specs=[VM] * 8 + [ANY] * 4,
-        out_specs=[VM] * len(small) + [ANY] * len(grads),
+        in_specs=[ANY] * 12,
+        out_specs=[ANY] * len(shapes),
         scratch_shapes=[pltpu.VMEM(s, d) for s, d in scratch]
         + [pltpu.SemaphoreType.DMA((SEMS,)), pltpu.SemaphoreType.DMA((SEMS,))],
         compiler_params=pltpu.CompilerParams(
@@ -682,9 +791,10 @@
     mixed, gres, dq, kg, vg, gg, dwout, dwgate, dwup, dwdown = pl.pallas_call(
         hand_over,
         out_shape=shapes,
-        in_specs=[VM] * len(shapes),
+        in_specs=[ANY] * len(shapes),
         out_specs=[ANY] * len(shapes),
-        scratch_shapes=[pltpu.SemaphoreType.DMA((len(shapes),))],
+        scratch_shapes=[pltpu.VMEM(s, d) for s, d in small + grads]
+        + [pltpu.SemaphoreType.DMA((len(shapes),))] * 2,
     )(*results)
     return (mixed, gres, dq, kg, vg, gg.reshape(4096), dwout, dwgate.T, dwup.T, dwdown)
 

time: 114 us -> 98.4 us (0.86)
  Pallas kernels: 112 us -> 97.5 us
    pallas_call x2, Pallas kernels: 112 us -> 97.5 us  [the longest x1 94.2 us: body(): pl.pallas_call(layer, out_shape=shapes, in_specs=[ANY] * 12, out_specs=[A...]
where the time goes in v4:
time: 98.4 us; the launch traced here: 98.3 us
  Pallas kernels  97.5 us (99%)
    pallas_call x1, Pallas kernels, body(): pl.pallas_call(layer, out_shape=shapes, in_specs=[ANY] * 12, out_specs=[A...  94.2 us
    pallas_call x1, Pallas kernels, body(): pl.pallas_call(hand_over, out_shape=shapes, in_specs=[ANY] * len(shapes),...  3.27 us

profile of v4, /device:TPU:1, one launch (start us, length us, event | category | flops | bytes accessed | tf_op | source)
XLA Modules:
  0.0 98.3 jit_solution(6236541411269356140)
XLA Ops:
  0.6 94.2 %shard_map.195 = (bf16[8,4096]{1,0:T(8,128)(2,1)}, bf16[8,4096]{1,0:T(8,128)(2,1)}, bf16[128,256]{1,0:T(8,128)(2,1)}, f32[8,1024]{1,0:T(8,128)}, f32[8,1024]{1,0...) custom-call(bf16[128,1024]{1,0:T(8,128)(2,1)} %keys_h.1, ...), custom_call_target="tpu_custom_call" | custom-call | tf_op jit(solution)/shard_map/pallas_call | solution.py:777
  94.8 3.3 %shard_map.196 = (bf16[8,4096]{1,0:T(8,128)(2,1)}, bf16[8,4096]{1,0:T(8,128)(2,1)}, bf16[128,256]{1,0:T(8,128)(2,1)}, f32[8,1024]{1,0:T(8,128)}, f32[8,1024]{1,0...) custom-call(bf16[8,4096]{1,0:T(8,128)(2,1)} %get-tuple-element.30.re, ...), custom_call_target="tpu_custom_call" | custom-call | tf_op jit(solution)/shard_map/pallas_call | solution.py:791
